TPU v7x, 32 devices: a whole 2x2x4 slice. The times are simulated.
32 devices in a mesh: user: 4 (over z), ctx: 2 (over y), head: 4 (over x, core).
Axes of the slice: x: 2, y: 2, z: 4, core: 2. Of those that a mesh axis runs over, the one named last changes fastest.
Arguments:
- catalog: bfloat16 [2048, 1024], P('user'), may hold values from -6 to 6
- cand_owner: int32 [4, 512, 1], P('user', 'ctx'), may hold values from 0 to 3; in each aligned block of 256 rows (0 to 255, 256 to 511, ..., all dimensions but the last counted through in order) at most 128 rows name the same one
- cand_row: int32 [4, 512], P('user', 'ctx'), may hold values from 0 to 511
- hist_len: int32 [4], P('user'), may hold values from 768 to 3072, as said below
- proj_weight: bfloat16 [1024, 2, 1024], P(None, None, 'head'), may hold values from -0.1875 to 0.1875
- keys: bfloat16 [4, 3072, 1024], P('user', 'ctx', 'head'), may hold values from -6 to 6
- values: bfloat16 [4, 3072, 1024], P('user', 'ctx', 'head'), may hold values from -640 to 640
- out_weight: bfloat16 [1024, 1024], P('head'), may hold values from -0.1875 to 0.1875
Outputs:
- ranked: bfloat16 [4, 512, 1024], P('user', 'ctx', 'head')
Inputs may be any that keep to these rules, and one draw needn't show every extreme that they name: `cand_owner`: within each aligned block of 256 shortlisted items of one user (one ctx index), at most 128 are owned by the same catalog shard. `hist_len`: at least one user has all 3072 events.
All inputs are finite; a program needn't handle non-finite values.
Results may differ from a plain program's by a relative error of at most 0.0071.
Values may be sent and summed in bfloat16 or wider, within the bound.
No kernel may reach another device: no remote copies, remote signals or barrier semaphores. Data moves between devices by JAX's collectives and lax.ppermute only.
A program may use at most 64 MiB of HBM per device.

v0:
```python
import functools

import jax
import jax.numpy as jnp
from jax import lax
from jax.experimental import pallas as pl
from jax.experimental.pallas import tpu as pltpu
from jax.sharding import PartitionSpec as P


HEAD = 128


def attend_block(query_rows, key_rows, value_rows, offset, length):
    row_total = query_rows.shape[0]
    key_total = key_rows.shape[0]
    head_count = query_rows.shape[1] // HEAD
    query_heads = query_rows.reshape(row_total, head_count, HEAD)
    key_heads = key_rows.reshape(key_total, head_count, HEAD)
    value_heads = value_rows.reshape(key_total, head_count, HEAD)
    scores = jnp.einsum(
        "rhc,nhc->rhn", query_heads, key_heads, preferred_element_type=jnp.float32
    ) * HEAD ** (-0.5)
    places = offset + jnp.arange(key_total, dtype=jnp.int32)
    weights = jnp.where(
        places[None, None, :] < length, jax.nn.silu(scores) / length.astype(jnp.float32), 0.0
    ).astype(jnp.bfloat16)
    mixed_rows = jnp.einsum(
        "rhn,nhc->rhc", weights, value_heads, preferred_element_type=jnp.float32
    )
    return mixed_rows.reshape(row_total, head_count * HEAD)


def event_split(catalog, cand_owner, cand_row, hist_len, proj_weight, keys, values, out_weight):
    user_count = lax.axis_size("user")
    owners = cand_owner[0, :, 0]
    wanted = cand_row[0]
    cand_count = wanted.shape[0]
    slot_count = 2 * cand_count // user_count
    model_width = catalog.shape[1]
    col_share = proj_weight.shape[2]
    owner_hot = (owners[:, None] == jnp.arange(user_count, dtype=jnp.int32)[None, :]).astype(
        jnp.int32
    )
    rank_in = jnp.sum(jnp.cumsum(owner_hot, axis=0) * owner_hot, axis=1) - 1
    places = owners * slot_count + rank_in
    request = (
        jnp.zeros((user_count * slot_count,), jnp.int32)
        .at[places]
        .set(wanted)
        .reshape(user_count, slot_count)
    )
    weight_flat = proj_weight.reshape(model_width, 2 * col_share)
    asked_ids = lax.all_to_all(request, "user", split_axis=0, concat_axis=0, tiled=True)
    picked = jax.nn.silu(
        jnp.dot(
            jnp.take(catalog, asked_ids.reshape(-1), axis=0),
            weight_flat,
            preferred_element_type=jnp.float32,
        )
    ).astype(jnp.bfloat16)
    served = picked.reshape(asked_ids.shape[0], asked_ids.shape[1], 2 * col_share)
    returned = lax.all_to_all(served, "user", split_axis=0, concat_axis=0, tiled=True)
    own_rows = jnp.take(returned.reshape(user_count * slot_count, 2 * col_share), places, axis=0)
    queries = own_rows[:, :col_share]
    gates = own_rows[:, col_share:]
    length = hist_len[0]
    key_rows = keys[0]
    value_rows = values[0]
    all_queries = lax.all_gather(queries, "ctx", axis=0, tiled=True)
    offset = lax.axis_index("ctx") * key_rows.shape[0]
    attended = lax.psum_scatter(
        attend_block(all_queries, key_rows, value_rows, offset, length),
        "ctx",
        scatter_dimension=0,
        tiled=True,
    )
    gated_rows = (attended * gates.astype(jnp.float32)).astype(jnp.bfloat16)
    partials = jnp.dot(gated_rows, out_weight, preferred_element_type=jnp.float32)
    ranked = lax.psum_scatter(partials, "head", scatter_dimension=1, tiled=True).astype(
        jnp.bfloat16
    )
    return ranked.reshape(1, cand_count, col_share)


def swap(x, axis, k):
    return lax.ppermute(x, axis, [(i, i ^ k) for i in range(lax.axis_size(axis))])


def columns_of(x, start, count):
    return lax.dynamic_slice_in_dim(x, start, count, 1)


def silu(x):
    half = 0.5 * x
    return half + half * jnp.tanh(half)


KEY_BLOCK = 256


def one_hot(condition):
    return jnp.where(condition, 1.0, 0.0).astype(jnp.bfloat16)


def shard_kernel(catalog_ref, weight_ref, query_ref, gate_ref):
    col_share, width = gate_ref.shape[1], query_ref.shape[1]
    cols = pl.ds(pl.multiple_of(lax.axis_index("ctx") * width, width), width)
    rows = catalog_ref[...]
    query = jnp.dot(rows, weight_ref[:, cols], preferred_element_type=jnp.float32)
    query_ref[...] = silu(query).astype(query_ref.dtype)
    gates = jnp.dot(rows, weight_ref[:, col_share:], preferred_element_type=jnp.float32)
    gates = silu(gates).astype(gate_ref.dtype)
    for part in range(col_share // width):
        cols = pl.ds(pl.multiple_of((lax.axis_index("ctx") ^ part) * width, width), width)
        gate_ref[:, cols] = gates[:, part * width : (part + 1) * width]


def project_shard(catalog, weight, width):
    shard_rows, model_width = catalog.shape
    col_share = weight.shape[1] // 2
    vmem = pl.BlockSpec(memory_space=pltpu.VMEM)
    return pl.pallas_call(
        shard_kernel,
        out_shape=[
            jax.ShapeDtypeStruct((shard_rows, width), jnp.bfloat16),
            jax.ShapeDtypeStruct((shard_rows, col_share), jnp.bfloat16),
        ],
        in_specs=[vmem, vmem],
        out_specs=[vmem, vmem],
        compiler_params=pltpu.CompilerParams(vmem_limit_bytes=16 << 20),
        cost_estimate=pl.CostEstimate(
            flops=2 * shard_rows * model_width * (col_share + width),
            transcendentals=shard_rows * (col_share + width),
            bytes_accessed=2 * model_width * (shard_rows + 2 * col_share),
        ),
    )(catalog, weight)


def store_gates(ref, base, hot, gates_ref):
    width, col_share = ref.shape[1], gates_ref.shape[1]
    count = hot.shape[0] * width // col_share
    rows = jnp.dot(hot[:count], gates_ref[...], preferred_element_type=jnp.float32)
    rows = rows.astype(ref.dtype)
    for part in range(col_share // width):
        ref[base + part * count : base + (part + 1) * count, :] = rows[
            :, part * width : (part + 1) * width
        ]


def serve_kernel(piece_count, user_count, slot_count, *refs):
    rows_ref, gates_ref, slots_ref, ranks_ref, *out_refs = refs[piece_count:]
    user = lax.axis_index("user")
    shard_rows = rows_ref.shape[0]
    ids = jnp.concatenate([ref[...] for ref in refs[:piece_count]], axis=0)
    item_count = ids.shape[1]
    served = ids - user * shard_rows
    mine = [one_hot((served >= 0) & (served < shard_rows))]
    for k in range(user_count):
        own = ids[0:1] - (user ^ k) * shard_rows
        mine.append(one_hot((own >= 0) & (own < shard_rows)))
    mine = jnp.concatenate(mine, axis=0)
    before = one_hot(
        lax.broadcasted_iota(jnp.int32, (item_count, item_count), 0)
        < lax.broadcasted_iota(jnp.int32, (item_count, item_count), 1)
    )
    rank = jnp.dot(mine, before, preferred_element_type=jnp.float32)
    asked = mine[user_count:].astype(jnp.float32)
    shard = lax.broadcasted_iota(jnp.int32, asked.shape, 0).astype(jnp.float32)
    ranks_ref[0:1] = jnp.sum(asked * rank[user_count:], axis=0, keepdims=True)
    ranks_ref[1:2] = jnp.sum(asked * shard, axis=0, keepdims=True)
    served = jnp.clip(served, 0, shard_rows - 1)
    slot = lax.broadcasted_iota(jnp.int32, (slot_count, item_count), 0).astype(jnp.float32)
    row = lax.broadcasted_iota(jnp.int32, (slot_count, shard_rows), 1)
    for k in (*range(1, user_count), 0):
        place = jnp.where(mine[k : k + 1] > 0, rank[k : k + 1], -1.0)
        parts = jnp.concatenate([served[k : k + 1] >> 8, served[k : k + 1] & 255], axis=0)
        found = lax.dot_general(
            one_hot(slot == place),
            parts.astype(jnp.float32).astype(jnp.bfloat16),
            (((1,), (1,)), ((), ())),
            preferred_element_type=jnp.float32,
        )
        at = (found[:, 0:1] * 256.0 + found[:, 1:2]).astype(jnp.int32)
        slots_ref[:, k : k + 1] = at
        if k > 0:
            hot = one_hot(row == at)
            out_refs[k - 1][:slot_count, :] = jnp.dot(
                hot, rows_ref[...], preferred_element_type=jnp.float32
            ).astype(jnp.bfloat16)
        if k == 1:
            store_gates(out_refs[0], slot_count, hot, gates_ref)


def serve(pieces, rows, gates, slot_count, width):
    user_count, item_count = sum(p.shape[0] for p in pieces), pieces[0].shape[1]
    vmem = pl.BlockSpec(memory_space=pltpu.VMEM)
    return pl.pallas_call(
        functools.partial(serve_kernel, len(pieces), user_count, slot_count),
        out_shape=[
            jax.ShapeDtypeStruct((slot_count, user_count), jnp.int32),
            jax.ShapeDtypeStruct((2, item_count), jnp.float32),
        ]
        + [
            jax.ShapeDtypeStruct((slot_count * (2 if k == 1 else 1), width), jnp.bfloat16)
            for k in range(1, user_count)
        ],
        in_specs=[vmem] * (len(pieces) + 2),
        out_specs=[vmem] * (user_count + 1),
        compiler_params=pltpu.CompilerParams(vmem_limit_bytes=16 << 20),
        cost_estimate=pl.CostEstimate(
            flops=2 * user_count * slot_count * rows.shape[0] * width,
            transcendentals=0,
            bytes_accessed=2 * rows.shape[0] * width,
        ),
    )(*pieces, rows, gates)


def serve_rest_kernel(user_count, slots_ref, ranks_ref, rows_ref, gates_ref, plan_ref, query_ref, *out_refs):
    shard_rows = rows_ref.shape[0]
    slot_count = query_ref.shape[0]
    row = lax.broadcasted_iota(jnp.int32, (slot_count, shard_rows), 1)
    for ref, k in zip(out_refs, (0, *range(2, user_count)), strict=True):
        hot = one_hot(row == slots_ref[:, k : k + 1])
        store_gates(ref, 0, hot, gates_ref)
        if k == 0:
            query_ref[...] = jnp.dot(
                hot, rows_ref[...], preferred_element_type=jnp.float32
            ).astype(jnp.bfloat16)
    item_count = ranks_ref.shape[1]
    same = one_hot(
        lax.broadcasted_iota(jnp.int32, (item_count, item_count), 0)
        == lax.broadcasted_iota(jnp.int32, (item_count, item_count), 1)
    )
    found = lax.dot_general(
        same,
        ranks_ref[...].astype(jnp.bfloat16),
        (((1,), (1,)), ((), ())),
        preferred_element_type=jnp.float32,
    )
    plan_ref[...] = (found[:, 0:1] + found[:, 1:2] * slot_count).astype(jnp.int32)


def serve_rest(slots, ranks, rows, gates):
    slot_count, user_count = slots.shape
    (shard_rows, width), col_share = rows.shape, gates.shape[1]
    count = user_count - (user_count > 1)
    vmem = pl.BlockSpec(memory_space=pltpu.VMEM)
    return pl.pallas_call(
        functools.partial(serve_rest_kernel, user_count),
        out_shape=[jax.ShapeDtypeStruct((ranks.shape[1], 1), jnp.int32)]
        + [jax.ShapeDtypeStruct((slot_count, width), jnp.bfloat16)] * (count + 1),
        in_specs=[vmem] * 4,
        out_specs=[vmem] * (count + 2),
        compiler_params=pltpu.CompilerParams(vmem_limit_bytes=16 << 20),
        cost_estimate=pl.CostEstimate(
            flops=2 * count * slot_count * shard_rows * width,
            transcendentals=0,
            bytes_accessed=2 * shard_rows * col_share,
        ),
    )(slots, ranks, rows, gates)


def pick(plan, stride, slot_rows):
    slot_count, width = slot_rows[0].shape
    slot = lax.broadcasted_iota(jnp.int32, (plan.shape[0], slot_count), 1)
    total = jnp.zeros((plan.shape[0], width), jnp.float32)
    for k, rows in enumerate(slot_rows):
        total += jnp.dot(
            one_hot(slot == plan - k * stride), rows, preferred_element_type=jnp.float32
        )
    return total


def attention_kernel(group, user_count, length_ref, plan_ref, *refs):
    query_refs, out_ref = refs[:user_count], refs[-1]
    key_ref, value_ref, *event_refs = refs[user_count:-1]
    ctx, length = lax.axis_index("ctx"), length_ref[...]
    item_count, width = out_ref.shape
    plan = plan_ref[group * item_count : (group + 1) * item_count, :]
    stride = query_refs[0].shape[0]
    query = pick(plan, stride, [ref[:stride, :] for ref in query_refs]).astype(jnp.bfloat16)
    event_count = key_ref.shape[0]
    scale = 0.5 * HEAD ** (-0.5)
    scale_len = scale / length.astype(jnp.float32)
    for head in range(width // HEAD):
        cols = slice(head * HEAD, (head + 1) * HEAD)
        total = jnp.zeros((item_count, HEAD), jnp.float32)
        for k in range(len(event_refs) + 1):
            first = (ctx ^ k) * event_count
            for start in range(0, event_count, KEY_BLOCK):
                stop = min(start + KEY_BLOCK, event_count)
                if k == 0:
                    at = pl.ds(pl.multiple_of(ctx * width + head * HEAD, HEAD), HEAD)
                    key, value = key_ref[start:stop, at], value_ref[start:stop, at]
                else:
                    key = event_refs[k - 1][start:stop, cols]
                    value = event_refs[k - 1][event_count + start : event_count + stop, cols]
                place = first + start + lax.broadcasted_iota(jnp.int32, value.shape, 0)
                value = jnp.where(place < length, value, jnp.zeros_like(value))
                raw = lax.dot_general(
                    query[:, cols],
                    key,
                    (((1,), (1,)), ((), ())),
                    preferred_element_type=jnp.float32,
                )
                lead = raw * scale_len
                weights = (lead + lead * jnp.tanh(raw * scale)).astype(jnp.bfloat16)
                total += jnp.dot(weights, value, preferred_element_type=jnp.float32)
        out_ref[:, cols] = total


def attend(length, plan, queries, keys, values, events, group):
    width = queries[0].shape[1]
    item_count = plan.shape[0] // (len(events) + 1)
    event_count = (len(events) + 1) * keys.shape[0]
    vmem = pl.BlockSpec(memory_space=pltpu.VMEM)
    operands = (length, plan, *queries, keys, values, *events)
    return pl.pallas_call(
        functools.partial(attention_kernel, group, len(queries)),
        out_shape=jax.ShapeDtypeStruct((item_count, width), jnp.float32),
        in_specs=[vmem] * len(operands),
        out_specs=vmem,
        compiler_params=pltpu.CompilerParams(vmem_limit_bytes=24 << 20),
        cost_estimate=pl.CostEstimate(
            flops=4 * item_count * event_count * width,
            transcendentals=item_count * event_count * (width // HEAD),
            bytes_accessed=4 * event_count * width,
        ),
    )(*operands)


def gate_kernel(part, part_count, stride, plan_ref, attended_ref, *refs):
    gate_refs, out_ref = refs[:-1], refs[-1]
    item_count = out_ref.shape[0]
    count = stride // part_count
    starts = [ref.shape[0] - stride + part * count for ref in gate_refs]
    slots = [ref[at : at + count, :] for at, ref in zip(starts, gate_refs, strict=True)]
    gates = pick(plan_ref[:item_count, :], stride, slots)
    out_ref[...] = (attended_ref[...] * gates).astype(out_ref.dtype)


def gate(plan, attended, gates, part, part_count):
    stride = gates[0].shape[0]
    vmem = pl.BlockSpec(memory_space=pltpu.VMEM)
    operands = (plan, attended, *gates)
    return pl.pallas_call(
        functools.partial(gate_kernel, part, part_count, stride),
        out_shape=jax.ShapeDtypeStruct(attended.shape, jnp.bfloat16),
        in_specs=[vmem] * len(operands),
        out_specs=vmem,
        compiler_params=pltpu.CompilerParams(vmem_limit_bytes=16 << 20),
        cost_estimate=pl.CostEstimate(
            flops=2 * attended.size * len(gates) * gates[0].shape[0],
            transcendentals=0,
            bytes_accessed=6 * attended.size,
        ),
    )(*operands)


def project_kernel(head_count, part, *refs):
    pieces, weights = refs[:head_count], refs[head_count : 2 * head_count]
    out_ref = refs[-1]
    width = pieces[0].shape[1]
    wanted = lax.axis_index("ctx") ^ part
    chosen = []
    for ref in weights:
        weight = ref[:width, :]
        for other in range(1, ref.shape[0] // width):
            rows = slice(other * width, (other + 1) * width)
            weight = jnp.where(wanted == other, ref[rows, :], weight)
        chosen.append(weight)
    total = jnp.dot(
        jnp.concatenate([piece[...] for piece in pieces], axis=1),
        jnp.concatenate(chosen, axis=0),
        preferred_element_type=jnp.float32,
    )
    if len(refs) > 2 * head_count + 1:
        total += refs[2 * head_count][...]
    out_ref[...] = total.astype(out_ref.dtype)


def project_out(pieces, weights, part, before, dtype):
    item_count, width = pieces[0].shape
    cols = weights[0].shape[1]
    vmem = pl.BlockSpec(memory_space=pltpu.VMEM)
    operands = (*pieces, *weights) + (() if before is None else (before,))
    return pl.pallas_call(
        functools.partial(project_kernel, len(pieces), part),
        out_shape=jax.ShapeDtypeStruct((item_count, cols), dtype),
        in_specs=[vmem] * len(operands),
        out_specs=vmem,
        compiler_params=pltpu.CompilerParams(vmem_limit_bytes=16 << 20),
        cost_estimate=pl.CostEstimate(
            flops=2 * item_count * cols * width * len(pieces),
            transcendentals=0,
            bytes_accessed=2 * cols * width * len(pieces),
        ),
    )(*operands)


def head_split(catalog, cand_owner, cand_row, hist_len, proj_weight, keys, values, out_weight):
    user_count, ctx_count = lax.axis_size("user"), lax.axis_size("ctx")
    head_count = lax.axis_size("head")
    ctx, head = lax.axis_index("ctx"), lax.axis_index("head")
    shard_rows, model_width = catalog.shape
    col_share = proj_weight.shape[2]
    width = col_share // ctx_count
    cand_count = cand_row.shape[1]
    slot_count = ctx_count * (2 * cand_count // user_count)
    key_rows, value_rows = keys[0], values[0]
    length = hist_len.reshape(1, 1)

    ids = cand_owner[0].reshape(1, cand_count) * shard_rows + cand_row
    others = [swap(ids, "ctx", k) for k in range(1, ctx_count)]
    pieces, step = [jnp.concatenate([ids, *others], axis=1)], 1
    while step < user_count:
        pieces.append(swap(jnp.concatenate(pieces, axis=0), "user", step))
        step *= 2

    events = []
    for k in range(1, ctx_count):
        at = (ctx ^ k) * width
        halves = [lax.dynamic_slice_in_dim(x, at, width, 1) for x in (key_rows, value_rows)]
        part = jnp.concatenate(halves, axis=0)
        events.append(swap(part, "ctx", k))

    weight = proj_weight.reshape(model_width, 2 * col_share)
    rows, gate_rows = project_shard(catalog, weight, width)
    slots, ranks, *served = serve(pieces, rows, gate_rows, slot_count, width)
    order = range(user_count - 1, 0, -1)
    fetched = {k: swap(served[k - 1], "user", k) for k in order}
    plan, query, *served = serve_rest(slots, ranks, rows, gate_rows)
    queries = [query] + [fetched[k] for k in range(1, user_count)]
    fetched = {k: swap(served[k - 1], "user", k) for k in order if k > 1}
    gates = [served[0], *queries[1:2]] + [fetched[k] for k in range(2, user_count)]

    weights = [columns_of(out_weight, head * col_share, col_share)]
    for j in range(1, head_count):
        part = columns_of(out_weight, (head ^ j) * col_share, col_share)
        weights.append(swap(part, "head", j))

    attended = [None] * ctx_count
    for k in range(ctx_count - 1, -1, -1):
        own = attend(length, plan, queries, key_rows, value_rows, events, k)
        attended[k] = swap(own, "ctx", k) if k > 0 else own

    ranked = None
    for k in range(ctx_count):
        gated = gate(plan, attended[k], gates, k, ctx_count)
        parts, bit = {0: gated}, head_count // 2
        while bit:
            for j in list(parts):
                parts[j ^ bit] = swap(parts[j], "head", bit)
            bit //= 2
        dtype = jnp.bfloat16 if k == ctx_count - 1 else jnp.float32
        heads = range(head_count)
        ranked = project_out(
            [parts[j] for j in heads], [weights[j] for j in heads], k, ranked, dtype
        )
    return ranked.reshape(1, cand_count, col_share)


def whole_heads(mesh, proj_weight):
    sizes = [mesh.shape[a] for a in ("user", "ctx", "head")]
    heads = proj_weight.shape[2] // mesh.shape["head"] // HEAD
    return all(n & (n - 1) == 0 for n in sizes) and heads % mesh.shape["ctx"] == 0 and sizes[0] > 1


def solution(mesh):
    def step(per_device):
        return jax.shard_map(
            per_device,
            mesh=mesh,
            in_specs=(
                P("user", None),
                P("user", "ctx", None),
                P("user", "ctx"),
                P("user"),
                P(None, None, "head"),
                P("user", "ctx", "head"),
                P("user", "ctx", "head"),
                P("head", None),
            ),
            out_specs=P("user", "ctx", "head"),
            check_vma=False,
        )

    def run(catalog, cand_owner, cand_row, hist_len, proj_weight, keys, values, out_weight):
        args = (catalog, cand_owner, cand_row, hist_len, proj_weight, keys, values, out_weight)
        if not whole_heads(mesh, proj_weight):
            return step(event_split)(*args)
        return step(head_split)(*args)

    return run
```

profile of v0, /device:TPU:0, one launch (start us, length us, event | category | flops | bytes accessed | tf_op | source)
XLA Modules:
  0.0 62.3 jit_solution(18365288776184639814)
XLA Ops:
  0.0 1.2 %dynamic-slice_bitcast_fusion = (bf16[1536,128]{1,0:T(8,128)(2,1)S(1)}, bf16[1536,128]{1,0:T(8,128)(2,1)S(1)}) fusion(bf16[1,1536,256]{2,1,0:T(8,128)(2,1)} %param.14, s32[]{:T(128)S(6)} %select_n.16, bf16[1,1536,256]{2,1,0:T(8,128)(2,1)} %param.13), kind=kLoop, calls=%fused_computation.1 | loop fusion | bytes 1572868 | tf_op jit(solution)/shard_map/dynamic_slice | solution.py:424
  1.2 0.0 copy-start.5
  1.2 0.0 copy-start.6
  1.2 0.0 copy-start.3
  1.2 1.0 %pad_maximum_fusion = bf16[3072,128]{1,0:T(8,128)(2,1)} fusion(bf16[1536,128]{1,0:T(8,128)(2,1)S(1)} %get-tuple-element.33, bf16[1536,128]{1,0:T(8,128)(2,1)S(1)} %get-tuple-element.34), kind=kLoop, calls=%fused_computation | loop fusion | flops 1572864 | bytes 1572864 | tf_op jit(solution)/shard_map/concatenate | solution.py:425
  2.2 3.0 %collective-permute-start.6 = (bf16[3072,128]{1,0:T(8,128)(2,1)}, bf16[3072,128]{1,0:T(8,128)(2,1)S(1)}, u32[]{:S(2)}, u32[]{:S(2)}) collective-permute-start(bf16[3072,128]{1,0:T(8,128)(2,1)} %pad_maximum_fusion), channel_id=1, source_target_pairs={{0,4},{4,0},{1,5},{5,1},{2,6},{6,2},{3,7},{7,3},{8,12},{12,8},{9,1... | collective-permute-start | bytes 2359304 | tf_op jit(solution)/shard_map/ppermute | solution.py:87
  5.2 0.1 collective-permute-start
  5.2 17.7 %collective-permute-done = s32[1,256]{1,0:T(1,128)S(1)} collective-permute-done((s32[1,256]{1,0:T(1,128)S(1)}, s32[1,256]{1,0:T(1,128)S(1)}, u32[]{:S(2)}, u32[]{:S(2)}) %collective-permute-start) | collective-permute-done | bytes 1056 | tf_op jit(solution)/shard_map/ppermute | solution.py:87
  23.0 1.8 %collective-permute-start.1 = (s32[1,512]{1,0:T(1,128)S(1)}, s32[1,512]{1,0:T(1,128)S(1)}, u32[]{:S(2)}, u32[]{:S(2)}) collective-permute-start(s32[1,512]{1,0:T(1,128)S(1)} %pad_add_fusion.1.refs_0_), channel_id=1, source_target_pairs={{0,8},{8,0},{16,24},{24,16},{1,9},{9,1},{17,25},{25,17},{2,10},{10... | collective-permute-start | bytes 6152 | tf_op jit(solution)/shard_map/ppermute | solution.py:87
  24.8 0.2 copy.9
  25.0 1.6 %collective-permute-done.1.refs_1_ = s32[1,512]{1,0:T(1,128)S(1)} collective-permute-done((s32[1,512]{1,0:T(1,128)S(1)}, s32[1,512]{1,0:T(1,128)S(1)}, u32[]{:S(2)}, u32[]{:S(2)}) %collective-permute-start.1) | collective-permute-done | bytes 2080 | tf_op jit(solution)/shard_map/ppermute | solution.py:87
  26.6 2.9 %collective-permute-start.2 = (s32[2,512]{1,0:T(2,128)S(1)}, s32[2,512]{1,0:T(2,128)S(1)}, u32[]{:S(2)}, u32[]{:S(2)}) collective-permute-start(s32[2,512]{1,0:T(2,128)S(1)} %pad_add_fusion), channel_id=1, source_target_pairs={{0,16},{8,24},{16,0},{24,8},{1,17},{9,25},{17,1},{25,9},{2,18},{10... | collective-permute-start | bytes 12296 | tf_op jit(solution)/shard_map/ppermute | solution.py:87
  29.4 0.8 %shard_map.82 = (bf16[512,128]{1,0:T(8,128)(2,1)S(1)}, bf16[512,256]{1,0:T(8,128)(2,1)S(1)}) custom-call(bf16[512,1024]{1,0:T(8,128)(2,1)S(1)} %copy-done.2, bf16[1024,512]{1,0:T(8,128)(2,1)S(1)} %bitcast.18), custom_call_target="tpu_custom_call" | custom-call | flops 402653184 | bytes 2097152 | tf_op jit(solution)/shard_map/pallas_call | solution.py:123
  30.2 0.0 copy-start
  30.2 0.9 %collective-permute-done.2.refs_2_ = s32[2,512]{1,0:T(2,128)S(1)} collective-permute-done((s32[2,512]{1,0:T(2,128)S(1)}, s32[2,512]{1,0:T(2,128)S(1)}, u32[]{:S(2)}, u32[]{:S(2)}) %collective-permute-start.2) | collective-permute-done | bytes 4128 | tf_op jit(solution)/shard_map/ppermute | solution.py:87
  31.1 1.4 %shard_map.83 = (s32[256,4]{1,0:T(8,128)S(1)}, f32[2,512]{1,0:T(2,128)S(1)}, bf16[512,128]{1,0:T(8,128)(2,1)S(1)}, bf16[256,128]{1,0:T(8,128)(2,1)S(1)}, bf16[256,128]{1,0:T(8,128)(2,1)S(1)}) custom-call(s32[1,512]{1,0:T(1,128)S(1)} %pad_add_fusion.1.refs_0_, s32[1,512]{1,0:T(1,128)S(1)} %collective-permute-done.1.refs_1_, ...), custom_call_target="tpu_custom_call" | custom-call | flops 134217728 | bytes 131072 | tf_op jit(solution)/shard_map/pallas_call | solution.py:198
  32.6 1.9 %collective-permute-start.3 = (bf16[512,128]{1,0:T(8,128)(2,1)S(1)}, bf16[512,128]{1,0:T(8,128)(2,1)S(1)}, u32[]{:S(2)}, u32[]{:S(2)}) collective-permute-start(bf16[512,128]{1,0:T(8,128)(2,1)S(1)} %get-tuple-element.23), channel_id=1, source_target_pairs={{0,8},{8,0},{16,24},{24,16},{1,9},{9,1},{17,25},{25,17},{2,10},{10... | collective-permute-start | bytes 393224 | tf_op jit(solution)/shard_map/ppermute | solution.py:87
  34.4 2.6 %collective-permute-start.4 = (bf16[256,128]{1,0:T(8,128)(2,1)S(1)}, bf16[256,128]{1,0:T(8,128)(2,1)S(1)}, u32[]{:S(2)}, u32[]{:S(2)}) collective-permute-start(bf16[256,128]{1,0:T(8,128)(2,1)S(1)} %get-tuple-element.24), channel_id=1, source_target_pairs={{0,16},{8,24},{16,0},{24,8},{1,17},{9,25},{17,1},{25,9},{2,18},{10... | collective-permute-start | bytes 196616 | tf_op jit(solution)/shard_map/ppermute | solution.py:87
  37.0 0.0 collective-permute-start.5
  37.7 0.6 shard_map.84
  38.3 2.0 %collective-permute-start.8 = (bf16[256,128]{1,0:T(8,128)(2,1)S(1)}, bf16[256,128]{1,0:T(8,128)(2,1)S(1)}, u32[]{:S(2)}, u32[]{:S(2)}) collective-permute-start(bf16[256,128]{1,0:T(8,128)(2,1)S(1)} %get-tuple-element.27), channel_id=1, source_target_pairs={{0,16},{8,24},{16,0},{24,8},{1,17},{9,25},{17,1},{25,9},{2,18},{10... | collective-permute-start | bytes 196616 | tf_op jit(solution)/shard_map/ppermute | solution.py:87
  40.3 0.4 collective-permute-done.4.refs_2_
  40.6 4.4 %collective-permute-start.9 = (bf16[256,128]{1,0:T(8,128)(2,1)S(1)}, bf16[256,128]{1,0:T(8,128)(2,1)S(1)}, u32[]{:S(2)}, u32[]{:S(2)}) collective-permute-start(bf16[256,128]{1,0:T(8,128)(2,1)S(1)} %get-tuple-element.28), channel_id=1, source_target_pairs={{0,24},{8,16},{16,8},{24,0},{1,25},{9,17},{17,9},{25,1},{2,26},{10... | collective-permute-start | bytes 196616 | tf_op jit(solution)/shard_map/ppermute | solution.py:87
  45.1 0.0 copy-start.4
  45.1 1.5 %shard_map.85 = f32[256,128]{1,0:T(8,128)S(1)} custom-call(s32[1,1]{1,0:T(1,128)} %bitcast.12.length_ref, s32[512,1]{1,0:T(8,128)S(1)} %get-tuple-element.21.plan_ref, bf16[256,128]{1,0:T(8,128)(2,1)S(1)} %get-tuple-element.22.refs_0_, bf16[512,128]{1,0:T(8,128)(2,1)S(1)} %collective-permute-done.3.refs_1_, ...), custom_call_target="tpu_custom_call" | custom-call | flops 402653184 | bytes 1572864 | tf_op jit(solution)/shard_map/pallas_call | solution.py:319
  46.6 1.6 %collective-permute-start.7 = (f32[256,128]{1,0:T(8,128)S(1)}, f32[256,128]{1,0:T(8,128)S(1)}, u32[]{:S(2)}, u32[]{:S(2)}) collective-permute-start(f32[256,128]{1,0:T(8,128)S(1)} %shard_map.85), channel_id=1, source_target_pairs={{0,4},{4,0},{1,5},{5,1},{2,6},{6,2},{3,7},{7,3},{8,12},{12,8},{9,1... | collective-permute-start | bytes 393224 | tf_op jit(solution)/shard_map/ppermute | solution.py:87
  48.2 0.1 constant_dynamic-slice_fusion
  48.3 0.1 collective-permute-start.13
  48.4 1.5 %collective-permute-start.14 = (bf16[256,256]{1,0:T(8,128)(2,1)S(1)}, bf16[256,256]{1,0:T(8,128)(2,1)S(1)}, u32[]{:S(2)}, u32[]{:S(2)}) collective-permute-start(bf16[256,256]{1,0:T(8,128)(2,1)S(1)} %get-tuple-element.32), channel_id=1, source_target_pairs={{0,2},{1,3},{2,0},{3,1},{4,6},{5,7},{6,4},{7,5},{8,10},{9,11},{10,... | collective-permute-start | bytes 393224 | tf_op jit(solution)/shard_map/ppermute | solution.py:87
  49.9 1.5 %shard_map.87.attended_ref = f32[256,128]{1,0:T(8,128)S(1)} custom-call(s32[1,1]{1,0:T(1,128)} %bitcast.13.length_ref, s32[512,1]{1,0:T(8,128)S(1)} %get-tuple-element.21.plan_ref, bf16[256,128]{1,0:T(8,128)(2,1)S(1)} %get-tuple-element.22.refs_0_, bf16[512,128]{1,0:T(8,128)(2,1)S(1)} %collective-permute-done.3.refs_1_, ...), custom_call_target="tpu_custom_call" | custom-call | flops 402653184 | bytes 1572864 | tf_op jit(solution)/shard_map/pallas_call | solution.py:319
  51.4 0.0 collective-permute-done.8.refs_2_
  51.5 0.4 collective-permute-start.15
  51.8 0.0 collective-permute-done.9.refs_3_
  51.8 0.3 shard_map.88.refs_0_
  52.2 1.5 %collective-permute-start.17 = (bf16[256,128]{1,0:T(8,128)(2,1)S(1)}, bf16[256,128]{1,0:T(8,128)(2,1)S(1)}, u32[]{:S(2)}, u32[]{:S(2)}) collective-permute-start(bf16[256,128]{1,0:T(8,128)(2,1)S(1)} %shard_map.88.refs_0_), channel_id=1, source_target_pairs={{0,2},{1,3},{2,0},{3,1},{4,6},{5,7},{6,4},{7,5},{8,10},{9,11},{10,... | collective-permute-start | bytes 196616 | tf_op jit(solution)/shard_map/ppermute | solution.py:87
  53.7 0.0 collective-permute-done.7.attended_ref
  53.7 0.3 shard_map.86.refs_0_
  54.0 0.6 collective-permute-start.11
  54.7 4.4 %collective-permute-done.17.refs_2_ = bf16[256,128]{1,0:T(8,128)(2,1)S(1)} collective-permute-done((bf16[256,128]{1,0:T(8,128)(2,1)S(1)}, bf16[256,128]{1,0:T(8,128)(2,1)S(1)}, u32[]{:S(2)}, u32[]{:S(2)}) %collective-permute-start.17) | collective-permute-done | bytes 65568 | tf_op jit(solution)/shard_map/ppermute | solution.py:87
  59.0 0.0 collective-permute-start.18
  59.0 0.0 collective-permute-done.14.refs_6_
  59.1 0.5 collective-permute-start.10
  59.6 0.6 collective-permute-done.11.refs_2_
  60.1 0.0 collective-permute-done.15.refs_7_
  60.1 0.2 collective-permute-done.18.refs_3_
  60.3 0.2 shard_map.89.refs_8_
  60.6 0.8 %collective-permute-done.12.refs_3_ = bf16[256,128]{1,0:T(8,128)(2,1)S(1)} collective-permute-done((bf16[256,128]{1,0:T(8,128)(2,1)S(1)}, bf16[256,128]{1,0:T(8,128)(2,1)S(1)}, u32[]{:S(2)}, u32[]{:S(2)}) %collective-permute-start.12) | collective-permute-done | bytes 65568 | tf_op jit(solution)/shard_map/ppermute | solution.py:87
  61.4 0.9 %shard_map.90 = bf16[256,256]{1,0:T(8,128)(2,1)} custom-call(bf16[256,128]{1,0:T(8,128)(2,1)S(1)} %shard_map.86.refs_0_, bf16[256,128]{1,0:T(8,128)(2,1)S(1)} %collective-permute-done.10.refs_1_, bf16[256,128]{1,0:T(8,128)(2,1)S(1)} %collective-permute-done.11.refs_2_, bf16[256,128]{1,0:T(8,128)(2,1)S(1)} %collective-permute-done.12.refs_3_, ...), custom_call_target="tpu_custom_call" | custom-call | flops 67108864 | bytes 262144 | tf_op jit(solution)/shard_map/pallas_call | solution.py:388
  (20 shorter events, 0.1 us)
Async XLA Ops:
  1.2 4.0 %copy-start.5 = (s32[1,256]{1,0:T(1,128)S(1)}, s32[1,256]{1,0:T(1,128)}, u32[]{:S(2)}) copy-start(s32[1,256]{1,0:T(1,128)} %param.10) | copy-start | bytes 3076
  1.2 4.0 %copy-start.6 = (s32[1,256,1]{1,2,0:T(1,128)S(1)}, s32[1,256,1]{1,2,0:T(1,128)}, u32[]{:S(2)}) copy-start(s32[1,256,1]{1,2,0:T(1,128)} %param.9) | copy-start | bytes 3076
  1.2 23.6 %copy-start.3 = (bf16[1024,2,256]{2,1,0:T(2,128)(2,1)S(1)}, bf16[1024,2,256]{2,1,0:T(2,128)(2,1)}, u32[]{:S(2)}) copy-start(bf16[1024,2,256]{2,1,0:T(2,128)(2,1)} %param.12) | copy-start | bytes 3145732
  2.2 42.9 %collective-permute-start.6 = (bf16[3072,128]{1,0:T(8,128)(2,1)}, bf16[3072,128]{1,0:T(8,128)(2,1)S(1)}, u32[]{:S(2)}, u32[]{:S(2)}) collective-permute-start(bf16[3072,128]{1,0:T(8,128)(2,1)} %pad_maximum_fusion), channel_id=1, source_target_pairs={{0,4},{4,0},{1,5},{5,1},{2,6},{6,2},{3,7},{7,3},{8,12},{12,8},{9,1... | collective-permute-start | bytes 2359304 | tf_op jit(solution)/shard_map/ppermute | solution.py:87
  5.2 17.8 %collective-permute-start = (s32[1,256]{1,0:T(1,128)S(1)}, s32[1,256]{1,0:T(1,128)S(1)}, u32[]{:S(2)}, u32[]{:S(2)}) collective-permute-start(s32[1,256]{1,0:T(1,128)S(1)} %bitcast_add_fusion), channel_id=1, source_target_pairs={{0,4},{4,0},{1,5},{5,1},{2,6},{6,2},{3,7},{7,3},{8,12},{12,8},{9,1... | collective-permute-start | bytes 3080 | tf_op jit(solution)/shard_map/ppermute | solution.py:87
  23.0 3.6 %collective-permute-start.1 = (s32[1,512]{1,0:T(1,128)S(1)}, s32[1,512]{1,0:T(1,128)S(1)}, u32[]{:S(2)}, u32[]{:S(2)}) collective-permute-start(s32[1,512]{1,0:T(1,128)S(1)} %pad_add_fusion.1.refs_0_), channel_id=1, source_target_pairs={{0,8},{8,0},{16,24},{24,16},{1,9},{9,1},{17,25},{25,17},{2,10},{10... | collective-permute-start | bytes 6152 | tf_op jit(solution)/shard_map/ppermute | solution.py:87
  24.8 4.7 %copy-start.2 = (bf16[512,1024]{1,0:T(8,128)(2,1)S(1)}, bf16[512,1024]{1,0:T(8,128)(2,1)}, u32[]{:S(2)}) copy-start(bf16[512,1024]{1,0:T(8,128)(2,1)} %catalog_ref.1) | copy-start | bytes 3145732
  26.6 4.6 %collective-permute-start.2 = (s32[2,512]{1,0:T(2,128)S(1)}, s32[2,512]{1,0:T(2,128)S(1)}, u32[]{:S(2)}, u32[]{:S(2)}) collective-permute-start(s32[2,512]{1,0:T(2,128)S(1)} %pad_add_fusion), channel_id=1, source_target_pairs={{0,16},{8,24},{16,0},{24,8},{1,17},{9,25},{17,1},{25,9},{2,18},{10... | collective-permute-start | bytes 12296 | tf_op jit(solution)/shard_map/ppermute | solution.py:87
  29.4 15.6 %copy-start.1 = (bf16[1,1536,256]{2,1,0:T(8,128)(2,1)S(1)}, bf16[1,1536,256]{2,1,0:T(8,128)(2,1)}, u32[]{:S(2)}) copy-start(bf16[1,1536,256]{2,1,0:T(8,128)(2,1)} %param.14) | copy-start | bytes 2359300
  30.2 14.9 %copy-start = (bf16[1,1536,256]{2,1,0:T(8,128)(2,1)S(1)}, bf16[1,1536,256]{2,1,0:T(8,128)(2,1)}, u32[]{:S(2)}) copy-start(bf16[1,1536,256]{2,1,0:T(8,128)(2,1)} %param.13) | copy-start | bytes 2359300
  32.6 12.5 %collective-permute-start.3 = (bf16[512,128]{1,0:T(8,128)(2,1)S(1)}, bf16[512,128]{1,0:T(8,128)(2,1)S(1)}, u32[]{:S(2)}, u32[]{:S(2)}) collective-permute-start(bf16[512,128]{1,0:T(8,128)(2,1)S(1)} %get-tuple-element.23), channel_id=1, source_target_pairs={{0,8},{8,0},{16,24},{24,16},{1,9},{9,1},{17,25},{25,17},{2,10},{10... | collective-permute-start | bytes 393224 | tf_op jit(solution)/shard_map/ppermute | solution.py:87
  34.4 6.2 %collective-permute-start.4 = (bf16[256,128]{1,0:T(8,128)(2,1)S(1)}, bf16[256,128]{1,0:T(8,128)(2,1)S(1)}, u32[]{:S(2)}, u32[]{:S(2)}) collective-permute-start(bf16[256,128]{1,0:T(8,128)(2,1)S(1)} %get-tuple-element.24), channel_id=1, source_target_pairs={{0,16},{8,24},{16,0},{24,8},{1,17},{9,25},{17,1},{25,9},{2,18},{10... | collective-permute-start | bytes 196616 | tf_op jit(solution)/shard_map/ppermute | solution.py:87
  37.0 8.0 %collective-permute-start.5 = (bf16[256,128]{1,0:T(8,128)(2,1)S(1)}, bf16[256,128]{1,0:T(8,128)(2,1)S(1)}, u32[]{:S(2)}, u32[]{:S(2)}) collective-permute-start(bf16[256,128]{1,0:T(8,128)(2,1)S(1)} %get-tuple-element.25), channel_id=1, source_target_pairs={{0,24},{8,16},{16,8},{24,0},{1,25},{9,17},{17,9},{25,1},{2,26},{10... | collective-permute-start | bytes 196616 | tf_op jit(solution)/shard_map/ppermute | solution.py:87
  38.3 13.2 %collective-permute-start.8 = (bf16[256,128]{1,0:T(8,128)(2,1)S(1)}, bf16[256,128]{1,0:T(8,128)(2,1)S(1)}, u32[]{:S(2)}, u32[]{:S(2)}) collective-permute-start(bf16[256,128]{1,0:T(8,128)(2,1)S(1)} %get-tuple-element.27), channel_id=1, source_target_pairs={{0,16},{8,24},{16,0},{24,8},{1,17},{9,25},{17,1},{25,9},{2,18},{10... | collective-permute-start | bytes 196616 | tf_op jit(solution)/shard_map/ppermute | solution.py:87
  40.6 11.2 %collective-permute-start.9 = (bf16[256,128]{1,0:T(8,128)(2,1)S(1)}, bf16[256,128]{1,0:T(8,128)(2,1)S(1)}, u32[]{:S(2)}, u32[]{:S(2)}) collective-permute-start(bf16[256,128]{1,0:T(8,128)(2,1)S(1)} %get-tuple-element.28), channel_id=1, source_target_pairs={{0,24},{8,16},{16,8},{24,0},{1,25},{9,17},{17,9},{25,1},{2,26},{10... | collective-permute-start | bytes 196616 | tf_op jit(solution)/shard_map/ppermute | solution.py:87
  45.1 3.1 %copy-start.4 = (bf16[256,1024]{1,0:T(8,128)(2,1)S(1)}, bf16[256,1024]{1,0:T(8,128)(2,1)}, u32[]{:S(2)}) copy-start(bf16[256,1024]{1,0:T(8,128)(2,1)} %param.15) | copy-start | bytes 1572868
  46.6 7.1 %collective-permute-start.7 = (f32[256,128]{1,0:T(8,128)S(1)}, f32[256,128]{1,0:T(8,128)S(1)}, u32[]{:S(2)}, u32[]{:S(2)}) collective-permute-start(f32[256,128]{1,0:T(8,128)S(1)} %shard_map.85), channel_id=1, source_target_pairs={{0,4},{4,0},{1,5},{5,1},{2,6},{6,2},{3,7},{7,3},{8,12},{12,8},{9,1... | collective-permute-start | bytes 393224 | tf_op jit(solution)/shard_map/ppermute | solution.py:87
  48.3 6.4 %collective-permute-start.13 = (bf16[256,256]{1,0:T(8,128)(2,1)S(1)}, bf16[256,256]{1,0:T(8,128)(2,1)S(1)}, u32[]{:S(2)}, u32[]{:S(2)}) collective-permute-start(bf16[256,256]{1,0:T(8,128)(2,1)S(1)} %get-tuple-element.30), channel_id=1, source_target_pairs={{0,1},{1,0},{2,3},{3,2},{4,5},{5,4},{6,7},{7,6},{8,9},{9,8},{10,11... | collective-permute-start | bytes 393224 | tf_op jit(solution)/shard_map/ppermute | solution.py:87
  48.4 10.7 %collective-permute-start.14 = (bf16[256,256]{1,0:T(8,128)(2,1)S(1)}, bf16[256,256]{1,0:T(8,128)(2,1)S(1)}, u32[]{:S(2)}, u32[]{:S(2)}) collective-permute-start(bf16[256,256]{1,0:T(8,128)(2,1)S(1)} %get-tuple-element.32), channel_id=1, source_target_pairs={{0,2},{1,3},{2,0},{3,1},{4,6},{5,7},{6,4},{7,5},{8,10},{9,11},{10,... | collective-permute-start | bytes 393224 | tf_op jit(solution)/shard_map/ppermute | solution.py:87
  51.5 8.7 %collective-permute-start.15 = (bf16[256,256]{1,0:T(8,128)(2,1)S(1)}, bf16[256,256]{1,0:T(8,128)(2,1)S(1)}, u32[]{:S(2)}, u32[]{:S(2)}) collective-permute-start(bf16[256,256]{1,0:T(8,128)(2,1)S(1)} %get-tuple-element.29), channel_id=1, source_target_pairs={{0,3},{1,2},{2,1},{3,0},{4,7},{5,6},{6,5},{7,4},{8,11},{9,10},{10,... | collective-permute-start | bytes 393224 | tf_op jit(solution)/shard_map/ppermute | solution.py:87
  52.2 6.9 %collective-permute-start.17 = (bf16[256,128]{1,0:T(8,128)(2,1)S(1)}, bf16[256,128]{1,0:T(8,128)(2,1)S(1)}, u32[]{:S(2)}, u32[]{:S(2)}) collective-permute-start(bf16[256,128]{1,0:T(8,128)(2,1)S(1)} %shard_map.88.refs_0_), channel_id=1, source_target_pairs={{0,2},{1,3},{2,0},{3,1},{4,6},{5,7},{6,4},{7,5},{8,10},{9,11},{10,... | collective-permute-start | bytes 196616 | tf_op jit(solution)/shard_map/ppermute | solution.py:87
  54.0 6.1 %collective-permute-start.11 = (bf16[256,128]{1,0:T(8,128)(2,1)S(1)}, bf16[256,128]{1,0:T(8,128)(2,1)S(1)}, u32[]{:S(2)}, u32[]{:S(2)}) collective-permute-start(bf16[256,128]{1,0:T(8,128)(2,1)S(1)} %shard_map.86.refs_0_), channel_id=1, source_target_pairs={{0,2},{1,3},{2,0},{3,1},{4,6},{5,7},{6,4},{7,5},{8,10},{9,11},{10,... | collective-permute-start | bytes 196616 | tf_op jit(solution)/shard_map/ppermute | solution.py:87
  54.7 5.5 %collective-permute-start.16 = (bf16[256,128]{1,0:T(8,128)(2,1)S(1)}, bf16[256,128]{1,0:T(8,128)(2,1)S(1)}, u32[]{:S(2)}, u32[]{:S(2)}) collective-permute-start(bf16[256,128]{1,0:T(8,128)(2,1)S(1)} %shard_map.88.refs_0_), channel_id=1, source_target_pairs={{0,1},{1,0},{2,3},{3,2},{4,5},{5,4},{6,7},{7,6},{8,9},{9,8},{10,11... | collective-permute-start | bytes 196616 | tf_op jit(solution)/shard_map/ppermute | solution.py:87
  59.0 1.3 %collective-permute-start.18 = (bf16[256,128]{1,0:T(8,128)(2,1)S(1)}, bf16[256,128]{1,0:T(8,128)(2,1)S(1)}, u32[]{:S(2)}, u32[]{:S(2)}) collective-permute-start(bf16[256,128]{1,0:T(8,128)(2,1)S(1)} %collective-permute-done.17.refs_2_), channel_id=1, source_target_pairs={{0,1},{1,0},{2,3},{3,2},{4,5},{5,4},{6,7},{7,6},{8,9},{9,8},{10,11... | collective-permute-start | bytes 196616 | tf_op jit(solution)/shard_map/ppermute | solution.py:87
  59.1 1.5 %collective-permute-start.10 = (bf16[256,128]{1,0:T(8,128)(2,1)S(1)}, bf16[256,128]{1,0:T(8,128)(2,1)S(1)}, u32[]{:S(2)}, u32[]{:S(2)}) collective-permute-start(bf16[256,128]{1,0:T(8,128)(2,1)S(1)} %shard_map.86.refs_0_), channel_id=1, source_target_pairs={{0,1},{1,0},{2,3},{3,2},{4,5},{5,4},{6,7},{7,6},{8,9},{9,8},{10,11... | collective-permute-start | bytes 196616 | tf_op jit(solution)/shard_map/ppermute | solution.py:87
  60.1 1.3 %collective-permute-start.12 = (bf16[256,128]{1,0:T(8,128)(2,1)S(1)}, bf16[256,128]{1,0:T(8,128)(2,1)S(1)}, u32[]{:S(2)}, u32[]{:S(2)}) collective-permute-start(bf16[256,128]{1,0:T(8,128)(2,1)S(1)} %collective-permute-done.11.refs_2_), channel_id=1, source_target_pairs={{0,1},{1,0},{2,3},{3,2},{4,5},{5,4},{6,7},{7,6},{8,9},{9,8},{10,11... | collective-permute-start | bytes 196616 | tf_op jit(solution)/shard_map/ppermute | solution.py:87
where the time goes:
time: 62.4 us; the launch traced here: 62.3 us
  waiting for transfers between devices  26.5 us (42%)
  starting transfers between devices  24.9 us (40%)
  Pallas kernels  7.58 us (12%)
  local copies, waits for them, and re-layouts  1.5 us (2%)
  other arithmetic  0.97 us (2%)
  between operations  0.83 us (1%)
    ppermute x19, waiting for transfers between devices, swap(): lax.ppermute(x, axis, [(i, i ^ k) for i in range(lax.axis_size(axis))])  26.5 us
    ppermute x19, starting transfers between devices, swap(): lax.ppermute(x, axis, [(i, i ^ k) for i in range(lax.axis_size(axis))])  24.9 us
    pallas_call x2, Pallas kernels, attend(): pl.pallas_call(functools.partial(attention_kernel, group, len(queries)),...  3.02 us
    pallas_call x1, Pallas kernels, serve(): pl.pallas_call(functools.partial(serve_kernel, len(pieces), user_count, s...  1.42 us
  transfers between devices with their start and end apart: 19, of which 8 were waited for; matrix products, arithmetic and copies ran while one was open for 0% of the time, Pallas kernels for 11%

commit v1 on v0

--- a/solution.py
+++ b/solution.py
@@ -97,10 +97,51 @@
 
 
 KEY_BLOCK = 256
+SPLIT = 3
 
 
 def one_hot(condition):
     return jnp.where(condition, 1.0, 0.0).astype(jnp.bfloat16)
+
+
+def split_kernel(partner, key_ref, value_ref, part_ref, held, read, written):
+    events, width = key_ref.shape[0], part_ref.shape[1]
+    cols = pl.ds(pl.multiple_of((lax.axis_index("ctx") ^ partner) * width, width), width)
+    step = pl.cdiv(events, SPLIT)
+    reads, writes = [], []
+    for half, ref in enumerate((key_ref, value_ref)):
+        for start in range(0, events, step):
+            rows = slice(start, min(start + step, events))
+            to = slice(half * events + rows.start, half * events + rows.stop)
+            n = len(reads)
+            reads.append(pltpu.make_async_copy(ref.at[rows, cols], held.at[to, :], read.at[n]))
+            writes.append(
+                pltpu.make_async_copy(held.at[to, :], part_ref.at[to, :], written.at[n])
+            )
+    for copy in reads:
+        copy.start()
+    for before, copy in zip(reads, writes, strict=True):
+        before.wait()
+        copy.start()
+    for copy in writes:
+        copy.wait()
+
+
+def split_events(key_rows, value_rows, width, partner):
+    events = key_rows.shape[0]
+    whole = pl.BlockSpec(memory_space=pl.ANY)
+    copies = pltpu.SemaphoreType.DMA((2 * SPLIT,))
+    return pl.pallas_call(
+        functools.partial(split_kernel, partner),
+        out_shape=jax.ShapeDtypeStruct((2 * events, width), key_rows.dtype),
+        in_specs=[whole, whole],
+        out_specs=whole,
+        scratch_shapes=[pltpu.VMEM((2 * events, width), key_rows.dtype), copies, copies],
+        compiler_params=pltpu.CompilerParams(vmem_limit_bytes=60 << 20),
+        cost_estimate=pl.CostEstimate(
+            flops=0, transcendentals=0, bytes_accessed=8 * events * width
+        ),
+    )(key_rows, value_rows)
 
 
 def shard_kernel(catalog_ref, weight_ref, query_ref, gate_ref):
@@ -402,7 +443,7 @@
 def head_split(catalog, cand_owner, cand_row, hist_len, proj_weight, keys, values, out_weight):
     user_count, ctx_count = lax.axis_size("user"), lax.axis_size("ctx")
     head_count = lax.axis_size("head")
-    ctx, head = lax.axis_index("ctx"), lax.axis_index("head")
+    head = lax.axis_index("head")
     shard_rows, model_width = catalog.shape
     col_share = proj_weight.shape[2]
     width = col_share // ctx_count
@@ -420,9 +461,7 @@
 
     events = []
     for k in range(1, ctx_count):
-        at = (ctx ^ k) * width
-        halves = [lax.dynamic_slice_in_dim(x, at, width, 1) for x in (key_rows, value_rows)]
-        part = jnp.concatenate(halves, axis=0)
+        part = split_events(key_rows, value_rows, width, k)
         events.append(swap(part, "ctx", k))
 
     weight = proj_weight.reshape(model_width, 2 * col_share)

time: 62.4 us -> 62.4 us (level)
  Pallas kernels: 7.58 us -> 9.64 us
  local copies, waits for them, and re-layouts: 1.5 us -> 0.32 us
  other arithmetic: 0.97 us -> 0.01 us
    pallas_call x0 -> x1, Pallas kernels: none -> 2.06 us  [split_events(): pl.pallas_call(functools.partial(split_kernel, partner), out_shape=jax.Sh...]
    dynamic_slice x1 -> x0, local copies, waits for them, and re-layouts: 1.17 us -> none  [head_split(): lax.dynamic_slice_in_dim(x, at, width, 1)]
    concatenate x1 -> x0, other arithmetic: 0.96 us -> none  [head_split(): part = jnp.concatenate(halves, axis=0)]
where the time goes in v1:
time: 62.4 us; the launch traced here: 62.3 us
  waiting for transfers between devices  26.5 us (42%)
  starting transfers between devices  24.9 us (40%)
  Pallas kernels  9.64 us (15%)
  between operations  0.82 us (1%)
    ppermute x19, waiting for transfers between devices, swap(): lax.ppermute(x, axis, [(i, i ^ k) for i in range(lax.axis_size(axis))])  26.5 us
    ppermute x19, starting transfers between devices, swap(): lax.ppermute(x, axis, [(i, i ^ k) for i in range(lax.axis_size(axis))])  24.9 us
    pallas_call x2, Pallas kernels, attend(): pl.pallas_call(functools.partial(attention_kernel, group, len(queries)),...  3.02 us
    pallas_call x1, Pallas kernels, split_events(): pl.pallas_call(functools.partial(split_kernel, partner), out_shape=jax.Sh...  2.06 us
    pallas_call x1, Pallas kernels, serve(): pl.pallas_call(functools.partial(serve_kernel, len(pieces), user_count, s...  1.42 us
  transfers between devices with their start and end apart: 19, of which 8 were waited for; matrix products, arithmetic and copies ran while one was open for 0% of the time, Pallas kernels for 11%

profile of v1, /device:TPU:0, one launch (start us, length us, event | category | flops | bytes accessed | tf_op | source)
XLA Modules:
  0.0 62.3 jit_solution(13413691310843110083)
XLA Ops:
  0.0 2.1 %shard_map.85 = bf16[3072,128]{1,0:T(8,128)(2,1)} custom-call(bf16[1536,256]{1,0:T(8,128)(2,1)} %bitcast.10, bf16[1536,256]{1,0:T(8,128)(2,1)} %bitcast.13), custom_call_target="tpu_custom_call" | custom-call | bytes 1572864 | tf_op jit(solution)/shard_map/pallas_call | solution.py:134
  2.1 3.1 %collective-permute-start.6 = (bf16[3072,128]{1,0:T(8,128)(2,1)}, bf16[3072,128]{1,0:T(8,128)(2,1)S(1)}, u32[]{:S(2)}, u32[]{:S(2)}) collective-permute-start(bf16[3072,128]{1,0:T(8,128)(2,1)} %shard_map.85), channel_id=1, source_target_pairs={{0,4},{4,0},{1,5},{5,1},{2,6},{6,2},{3,7},{7,3},{8,12},{12,8},{9,1... | collective-permute-start | bytes 2359304 | tf_op jit(solution)/shard_map/ppermute | solution.py:87
  5.2 0.1 collective-permute-start
  5.3 17.7 %collective-permute-done = s32[1,256]{1,0:T(1,128)S(1)} collective-permute-done((s32[1,256]{1,0:T(1,128)S(1)}, s32[1,256]{1,0:T(1,128)S(1)}, u32[]{:S(2)}, u32[]{:S(2)}) %collective-permute-start) | collective-permute-done | bytes 1056 | tf_op jit(solution)/shard_map/ppermute | solution.py:87
  23.0 1.8 %collective-permute-start.1 = (s32[1,512]{1,0:T(1,128)S(1)}, s32[1,512]{1,0:T(1,128)S(1)}, u32[]{:S(2)}, u32[]{:S(2)}) collective-permute-start(s32[1,512]{1,0:T(1,128)S(1)} %pad_add_fusion.1.refs_0_), channel_id=1, source_target_pairs={{0,8},{8,0},{16,24},{24,16},{1,9},{9,1},{17,25},{25,17},{2,10},{10... | collective-permute-start | bytes 6152 | tf_op jit(solution)/shard_map/ppermute | solution.py:87
  24.8 0.2 copy.9
  25.0 1.6 %collective-permute-done.1.refs_1_ = s32[1,512]{1,0:T(1,128)S(1)} collective-permute-done((s32[1,512]{1,0:T(1,128)S(1)}, s32[1,512]{1,0:T(1,128)S(1)}, u32[]{:S(2)}, u32[]{:S(2)}) %collective-permute-start.1) | collective-permute-done | bytes 2080 | tf_op jit(solution)/shard_map/ppermute | solution.py:87
  26.6 2.9 %collective-permute-start.2 = (s32[2,512]{1,0:T(2,128)S(1)}, s32[2,512]{1,0:T(2,128)S(1)}, u32[]{:S(2)}, u32[]{:S(2)}) collective-permute-start(s32[2,512]{1,0:T(2,128)S(1)} %pad_add_fusion), channel_id=1, source_target_pairs={{0,16},{8,24},{16,0},{24,8},{1,17},{9,25},{17,1},{25,9},{2,18},{10... | collective-permute-start | bytes 12296 | tf_op jit(solution)/shard_map/ppermute | solution.py:87
  29.4 0.8 %shard_map.82 = (bf16[512,128]{1,0:T(8,128)(2,1)S(1)}, bf16[512,256]{1,0:T(8,128)(2,1)S(1)}) custom-call(bf16[512,1024]{1,0:T(8,128)(2,1)S(1)} %copy-done.2, bf16[1024,512]{1,0:T(8,128)(2,1)S(1)} %bitcast.16), custom_call_target="tpu_custom_call" | custom-call | flops 402653184 | bytes 2097152 | tf_op jit(solution)/shard_map/pallas_call | solution.py:164
  30.2 0.0 copy-start
  30.2 0.9 %collective-permute-done.2.refs_2_ = s32[2,512]{1,0:T(2,128)S(1)} collective-permute-done((s32[2,512]{1,0:T(2,128)S(1)}, s32[2,512]{1,0:T(2,128)S(1)}, u32[]{:S(2)}, u32[]{:S(2)}) %collective-permute-start.2) | collective-permute-done | bytes 4128 | tf_op jit(solution)/shard_map/ppermute | solution.py:87
  31.1 1.4 %shard_map.83 = (s32[256,4]{1,0:T(8,128)S(1)}, f32[2,512]{1,0:T(2,128)S(1)}, bf16[512,128]{1,0:T(8,128)(2,1)S(1)}, bf16[256,128]{1,0:T(8,128)(2,1)S(1)}, bf16[256,128]{1,0:T(8,128)(2,1)S(1)}) custom-call(s32[1,512]{1,0:T(1,128)S(1)} %pad_add_fusion.1.refs_0_, s32[1,512]{1,0:T(1,128)S(1)} %collective-permute-done.1.refs_1_, ...), custom_call_target="tpu_custom_call" | custom-call | flops 134217728 | bytes 131072 | tf_op jit(solution)/shard_map/pallas_call | solution.py:239
  32.6 1.9 %collective-permute-start.3 = (bf16[512,128]{1,0:T(8,128)(2,1)S(1)}, bf16[512,128]{1,0:T(8,128)(2,1)S(1)}, u32[]{:S(2)}, u32[]{:S(2)}) collective-permute-start(bf16[512,128]{1,0:T(8,128)(2,1)S(1)} %get-tuple-element.23), channel_id=1, source_target_pairs={{0,8},{8,0},{16,24},{24,16},{1,9},{9,1},{17,25},{25,17},{2,10},{10... | collective-permute-start | bytes 393224 | tf_op jit(solution)/shard_map/ppermute | solution.py:87
  34.4 2.6 %collective-permute-start.4 = (bf16[256,128]{1,0:T(8,128)(2,1)S(1)}, bf16[256,128]{1,0:T(8,128)(2,1)S(1)}, u32[]{:S(2)}, u32[]{:S(2)}) collective-permute-start(bf16[256,128]{1,0:T(8,128)(2,1)S(1)} %get-tuple-element.24), channel_id=1, source_target_pairs={{0,16},{8,24},{16,0},{24,8},{1,17},{9,25},{17,1},{25,9},{2,18},{10... | collective-permute-start | bytes 196616 | tf_op jit(solution)/shard_map/ppermute | solution.py:87
  37.0 0.0 collective-permute-start.5
  37.7 0.6 shard_map.84
  38.3 2.0 %collective-permute-start.8 = (bf16[256,128]{1,0:T(8,128)(2,1)S(1)}, bf16[256,128]{1,0:T(8,128)(2,1)S(1)}, u32[]{:S(2)}, u32[]{:S(2)}) collective-permute-start(bf16[256,128]{1,0:T(8,128)(2,1)S(1)} %get-tuple-element.27), channel_id=1, source_target_pairs={{0,16},{8,24},{16,0},{24,8},{1,17},{9,25},{17,1},{25,9},{2,18},{10... | collective-permute-start | bytes 196616 | tf_op jit(solution)/shard_map/ppermute | solution.py:87
  40.2 0.4 collective-permute-done.4.refs_2_
  40.6 4.4 %collective-permute-start.9 = (bf16[256,128]{1,0:T(8,128)(2,1)S(1)}, bf16[256,128]{1,0:T(8,128)(2,1)S(1)}, u32[]{:S(2)}, u32[]{:S(2)}) collective-permute-start(bf16[256,128]{1,0:T(8,128)(2,1)S(1)} %get-tuple-element.28), channel_id=1, source_target_pairs={{0,24},{8,16},{16,8},{24,0},{1,25},{9,17},{17,9},{25,1},{2,26},{10... | collective-permute-start | bytes 196616 | tf_op jit(solution)/shard_map/ppermute | solution.py:87
  45.0 0.0 collective-permute-done.5.refs_3_
  45.1 0.0 collective-permute-done.3.refs_1_
  45.1 0.0 collective-permute-done.6.refs_6_
  45.1 0.0 copy-start.4
  45.1 1.5 %shard_map.86 = f32[256,128]{1,0:T(8,128)S(1)} custom-call(s32[1,1]{1,0:T(1,128)} %bitcast.8.length_ref, s32[512,1]{1,0:T(8,128)S(1)} %get-tuple-element.21.plan_ref, bf16[256,128]{1,0:T(8,128)(2,1)S(1)} %get-tuple-element.22.refs_0_, bf16[512,128]{1,0:T(8,128)(2,1)S(1)} %collective-permute-done.3.refs_1_, ...), custom_call_target="tpu_custom_call" | custom-call | flops 402653184 | bytes 1572864 | tf_op jit(solution)/shard_map/pallas_call | solution.py:360
  46.6 1.6 %collective-permute-start.7 = (f32[256,128]{1,0:T(8,128)S(1)}, f32[256,128]{1,0:T(8,128)S(1)}, u32[]{:S(2)}, u32[]{:S(2)}) collective-permute-start(f32[256,128]{1,0:T(8,128)S(1)} %shard_map.86), channel_id=1, source_target_pairs={{0,4},{4,0},{1,5},{5,1},{2,6},{6,2},{3,7},{7,3},{8,12},{12,8},{9,1... | collective-permute-start | bytes 393224 | tf_op jit(solution)/shard_map/ppermute | solution.py:87
  48.2 0.1 constant_dynamic-slice_fusion
  48.3 0.1 collective-permute-start.13
  48.4 1.5 %collective-permute-start.14 = (bf16[256,256]{1,0:T(8,128)(2,1)S(1)}, bf16[256,256]{1,0:T(8,128)(2,1)S(1)}, u32[]{:S(2)}, u32[]{:S(2)}) collective-permute-start(bf16[256,256]{1,0:T(8,128)(2,1)S(1)} %get-tuple-element.32), channel_id=1, source_target_pairs={{0,2},{1,3},{2,0},{3,1},{4,6},{5,7},{6,4},{7,5},{8,10},{9,11},{10,... | collective-permute-start | bytes 393224 | tf_op jit(solution)/shard_map/ppermute | solution.py:87
  49.9 1.5 %shard_map.88.attended_ref = f32[256,128]{1,0:T(8,128)S(1)} custom-call(s32[1,1]{1,0:T(1,128)} %bitcast.9.length_ref, s32[512,1]{1,0:T(8,128)S(1)} %get-tuple-element.21.plan_ref, bf16[256,128]{1,0:T(8,128)(2,1)S(1)} %get-tuple-element.22.refs_0_, bf16[512,128]{1,0:T(8,128)(2,1)S(1)} %collective-permute-done.3.refs_1_, ...), custom_call_target="tpu_custom_call" | custom-call | flops 402653184 | bytes 1572864 | tf_op jit(solution)/shard_map/pallas_call | solution.py:360
  51.4 0.0 collective-permute-done.8.refs_2_
  51.4 0.4 collective-permute-start.15
  51.8 0.0 collective-permute-done.9.refs_3_
  51.8 0.3 shard_map.89.refs_0_
  52.1 1.5 %collective-permute-start.17 = (bf16[256,128]{1,0:T(8,128)(2,1)S(1)}, bf16[256,128]{1,0:T(8,128)(2,1)S(1)}, u32[]{:S(2)}, u32[]{:S(2)}) collective-permute-start(bf16[256,128]{1,0:T(8,128)(2,1)S(1)} %shard_map.89.refs_0_), channel_id=1, source_target_pairs={{0,2},{1,3},{2,0},{3,1},{4,6},{5,7},{6,4},{7,5},{8,10},{9,11},{10,... | collective-permute-start | bytes 196616 | tf_op jit(solution)/shard_map/ppermute | solution.py:87
  53.7 0.0 collective-permute-done.7.attended_ref
  53.7 0.3 shard_map.87.refs_0_
  54.0 0.6 collective-permute-start.11
  54.6 0.0 collective-permute-done.13.refs_5_
  54.6 0.0 collective-permute-start.16
  54.6 4.4 %collective-permute-done.17.refs_2_ = bf16[256,128]{1,0:T(8,128)(2,1)S(1)} collective-permute-done((bf16[256,128]{1,0:T(8,128)(2,1)S(1)}, bf16[256,128]{1,0:T(8,128)(2,1)S(1)}, u32[]{:S(2)}, u32[]{:S(2)}) %collective-permute-start.17) | collective-permute-done | bytes 65568 | tf_op jit(solution)/shard_map/ppermute | solution.py:87
  59.0 0.0 collective-permute-start.18
  59.0 0.0 collective-permute-done.14.refs_6_
  59.0 0.5 collective-permute-start.10
  59.5 0.6 collective-permute-done.11.refs_2_
  60.1 0.2 collective-permute-done.18.refs_3_
  60.3 0.2 shard_map.90.refs_8_
  60.5 0.8 %collective-permute-done.12.refs_3_ = bf16[256,128]{1,0:T(8,128)(2,1)S(1)} collective-permute-done((bf16[256,128]{1,0:T(8,128)(2,1)S(1)}, bf16[256,128]{1,0:T(8,128)(2,1)S(1)}, u32[]{:S(2)}, u32[]{:S(2)}) %collective-permute-start.12) | collective-permute-done | bytes 65568 | tf_op jit(solution)/shard_map/ppermute | solution.py:87
  61.4 0.9 %shard_map.91 = bf16[256,256]{1,0:T(8,128)(2,1)} custom-call(bf16[256,128]{1,0:T(8,128)(2,1)S(1)} %shard_map.87.refs_0_, bf16[256,128]{1,0:T(8,128)(2,1)S(1)} %collective-permute-done.10.refs_1_, bf16[256,128]{1,0:T(8,128)(2,1)S(1)} %collective-permute-done.11.refs_2_, bf16[256,128]{1,0:T(8,128)(2,1)S(1)} %collective-permute-done.12.refs_3_, ...), custom_call_target="tpu_custom_call" | custom-call | flops 67108864 | bytes 262144 | tf_op jit(solution)/shard_map/pallas_call | solution.py:429
  (19 shorter events, 0.0 us)
Async XLA Ops:
  0.0 5.2 %copy-start.5 = (s32[1,256]{1,0:T(1,128)S(1)}, s32[1,256]{1,0:T(1,128)}, u32[]{:S(2)}) copy-start(s32[1,256]{1,0:T(1,128)} %param.10) | copy-start | bytes 3076
  0.0 5.2 %copy-start.6 = (s32[1,256,1]{1,2,0:T(1,128)S(1)}, s32[1,256,1]{1,2,0:T(1,128)}, u32[]{:S(2)}) copy-start(s32[1,256,1]{1,2,0:T(1,128)} %param.9) | copy-start | bytes 3076
  0.0 24.8 %copy-start.3 = (bf16[1024,2,256]{2,1,0:T(2,128)(2,1)S(1)}, bf16[1024,2,256]{2,1,0:T(2,128)(2,1)}, u32[]{:S(2)}) copy-start(bf16[1024,2,256]{2,1,0:T(2,128)(2,1)} %param.12) | copy-start | bytes 3145732
  2.1 43.0 %collective-permute-start.6 = (bf16[3072,128]{1,0:T(8,128)(2,1)}, bf16[3072,128]{1,0:T(8,128)(2,1)S(1)}, u32[]{:S(2)}, u32[]{:S(2)}) collective-permute-start(bf16[3072,128]{1,0:T(8,128)(2,1)} %shard_map.85), channel_id=1, source_target_pairs={{0,4},{4,0},{1,5},{5,1},{2,6},{6,2},{3,7},{7,3},{8,12},{12,8},{9,1... | collective-permute-start | bytes 2359304 | tf_op jit(solution)/shard_map/ppermute | solution.py:87
  5.2 17.8 %collective-permute-start = (s32[1,256]{1,0:T(1,128)S(1)}, s32[1,256]{1,0:T(1,128)S(1)}, u32[]{:S(2)}, u32[]{:S(2)}) collective-permute-start(s32[1,256]{1,0:T(1,128)S(1)} %bitcast_add_fusion), channel_id=1, source_target_pairs={{0,4},{4,0},{1,5},{5,1},{2,6},{6,2},{3,7},{7,3},{8,12},{12,8},{9,1... | collective-permute-start | bytes 3080 | tf_op jit(solution)/shard_map/ppermute | solution.py:87
  23.0 3.6 %collective-permute-start.1 = (s32[1,512]{1,0:T(1,128)S(1)}, s32[1,512]{1,0:T(1,128)S(1)}, u32[]{:S(2)}, u32[]{:S(2)}) collective-permute-start(s32[1,512]{1,0:T(1,128)S(1)} %pad_add_fusion.1.refs_0_), channel_id=1, source_target_pairs={{0,8},{8,0},{16,24},{24,16},{1,9},{9,1},{17,25},{25,17},{2,10},{10... | collective-permute-start | bytes 6152 | tf_op jit(solution)/shard_map/ppermute | solution.py:87
  24.8 4.7 %copy-start.2 = (bf16[512,1024]{1,0:T(8,128)(2,1)S(1)}, bf16[512,1024]{1,0:T(8,128)(2,1)}, u32[]{:S(2)}) copy-start(bf16[512,1024]{1,0:T(8,128)(2,1)} %catalog_ref.1) | copy-start | bytes 3145732
  26.6 4.6 %collective-permute-start.2 = (s32[2,512]{1,0:T(2,128)S(1)}, s32[2,512]{1,0:T(2,128)S(1)}, u32[]{:S(2)}, u32[]{:S(2)}) collective-permute-start(s32[2,512]{1,0:T(2,128)S(1)} %pad_add_fusion), channel_id=1, source_target_pairs={{0,16},{8,24},{16,0},{24,8},{1,17},{9,25},{17,1},{25,9},{2,18},{10... | collective-permute-start | bytes 12296 | tf_op jit(solution)/shard_map/ppermute | solution.py:87
  29.4 15.6 %copy-start.1 = (bf16[1,1536,256]{2,1,0:T(8,128)(2,1)S(1)}, bf16[1,1536,256]{2,1,0:T(8,128)(2,1)}, u32[]{:S(2)}) copy-start(bf16[1,1536,256]{2,1,0:T(8,128)(2,1)} %param.14) | copy-start | bytes 2359300
  30.2 14.9 %copy-start = (bf16[1,1536,256]{2,1,0:T(8,128)(2,1)S(1)}, bf16[1,1536,256]{2,1,0:T(8,128)(2,1)}, u32[]{:S(2)}) copy-start(bf16[1,1536,256]{2,1,0:T(8,128)(2,1)} %param.13) | copy-start | bytes 2359300
  32.6 12.5 %collective-permute-start.3 = (bf16[512,128]{1,0:T(8,128)(2,1)S(1)}, bf16[512,128]{1,0:T(8,128)(2,1)S(1)}, u32[]{:S(2)}, u32[]{:S(2)}) collective-permute-start(bf16[512,128]{1,0:T(8,128)(2,1)S(1)} %get-tuple-element.23), channel_id=1, source_target_pairs={{0,8},{8,0},{16,24},{24,16},{1,9},{9,1},{17,25},{25,17},{2,10},{10... | collective-permute-start | bytes 393224 | tf_op jit(solution)/shard_map/ppermute | solution.py:87
  34.4 6.2 %collective-permute-start.4 = (bf16[256,128]{1,0:T(8,128)(2,1)S(1)}, bf16[256,128]{1,0:T(8,128)(2,1)S(1)}, u32[]{:S(2)}, u32[]{:S(2)}) collective-permute-start(bf16[256,128]{1,0:T(8,128)(2,1)S(1)} %get-tuple-element.24), channel_id=1, source_target_pairs={{0,16},{8,24},{16,0},{24,8},{1,17},{9,25},{17,1},{25,9},{2,18},{10... | collective-permute-start | bytes 196616 | tf_op jit(solution)/shard_map/ppermute | solution.py:87
  37.0 8.0 %collective-permute-start.5 = (bf16[256,128]{1,0:T(8,128)(2,1)S(1)}, bf16[256,128]{1,0:T(8,128)(2,1)S(1)}, u32[]{:S(2)}, u32[]{:S(2)}) collective-permute-start(bf16[256,128]{1,0:T(8,128)(2,1)S(1)} %get-tuple-element.25), channel_id=1, source_target_pairs={{0,24},{8,16},{16,8},{24,0},{1,25},{9,17},{17,9},{25,1},{2,26},{10... | collective-permute-start | bytes 196616 | tf_op jit(solution)/shard_map/ppermute | solution.py:87
  38.3 13.2 %collective-permute-start.8 = (bf16[256,128]{1,0:T(8,128)(2,1)S(1)}, bf16[256,128]{1,0:T(8,128)(2,1)S(1)}, u32[]{:S(2)}, u32[]{:S(2)}) collective-permute-start(bf16[256,128]{1,0:T(8,128)(2,1)S(1)} %get-tuple-element.27), channel_id=1, source_target_pairs={{0,16},{8,24},{16,0},{24,8},{1,17},{9,25},{17,1},{25,9},{2,18},{10... | collective-permute-start | bytes 196616 | tf_op jit(solution)/shard_map/ppermute | solution.py:87
  40.6 11.2 %collective-permute-start.9 = (bf16[256,128]{1,0:T(8,128)(2,1)S(1)}, bf16[256,128]{1,0:T(8,128)(2,1)S(1)}, u32[]{:S(2)}, u32[]{:S(2)}) collective-permute-start(bf16[256,128]{1,0:T(8,128)(2,1)S(1)} %get-tuple-element.28), channel_id=1, source_target_pairs={{0,24},{8,16},{16,8},{24,0},{1,25},{9,17},{17,9},{25,1},{2,26},{10... | collective-permute-start | bytes 196616 | tf_op jit(solution)/shard_map/ppermute | solution.py:87
  45.1 3.1 %copy-start.4 = (bf16[256,1024]{1,0:T(8,128)(2,1)S(1)}, bf16[256,1024]{1,0:T(8,128)(2,1)}, u32[]{:S(2)}) copy-start(bf16[256,1024]{1,0:T(8,128)(2,1)} %param.15) | copy-start | bytes 1572868
  46.6 7.1 %collective-permute-start.7 = (f32[256,128]{1,0:T(8,128)S(1)}, f32[256,128]{1,0:T(8,128)S(1)}, u32[]{:S(2)}, u32[]{:S(2)}) collective-permute-start(f32[256,128]{1,0:T(8,128)S(1)} %shard_map.86), channel_id=1, source_target_pairs={{0,4},{4,0},{1,5},{5,1},{2,6},{6,2},{3,7},{7,3},{8,12},{12,8},{9,1... | collective-permute-start | bytes 393224 | tf_op jit(solution)/shard_map/ppermute | solution.py:87
  48.3 6.4 %collective-permute-start.13 = (bf16[256,256]{1,0:T(8,128)(2,1)S(1)}, bf16[256,256]{1,0:T(8,128)(2,1)S(1)}, u32[]{:S(2)}, u32[]{:S(2)}) collective-permute-start(bf16[256,256]{1,0:T(8,128)(2,1)S(1)} %get-tuple-element.30), channel_id=1, source_target_pairs={{0,1},{1,0},{2,3},{3,2},{4,5},{5,4},{6,7},{7,6},{8,9},{9,8},{10,11... | collective-permute-start | bytes 393224 | tf_op jit(solution)/shard_map/ppermute | solution.py:87
  48.4 10.7 %collective-permute-start.14 = (bf16[256,256]{1,0:T(8,128)(2,1)S(1)}, bf16[256,256]{1,0:T(8,128)(2,1)S(1)}, u32[]{:S(2)}, u32[]{:S(2)}) collective-permute-start(bf16[256,256]{1,0:T(8,128)(2,1)S(1)} %get-tuple-element.32), channel_id=1, source_target_pairs={{0,2},{1,3},{2,0},{3,1},{4,6},{5,7},{6,4},{7,5},{8,10},{9,11},{10,... | collective-permute-start | bytes 393224 | tf_op jit(solution)/shard_map/ppermute | solution.py:87
  51.4 8.7 %collective-permute-start.15 = (bf16[256,256]{1,0:T(8,128)(2,1)S(1)}, bf16[256,256]{1,0:T(8,128)(2,1)S(1)}, u32[]{:S(2)}, u32[]{:S(2)}) collective-permute-start(bf16[256,256]{1,0:T(8,128)(2,1)S(1)} %get-tuple-element.29), channel_id=1, source_target_pairs={{0,3},{1,2},{2,1},{3,0},{4,7},{5,6},{6,5},{7,4},{8,11},{9,10},{10,... | collective-permute-start | bytes 393224 | tf_op jit(solution)/shard_map/ppermute | solution.py:87
  52.1 6.9 %collective-permute-start.17 = (bf16[256,128]{1,0:T(8,128)(2,1)S(1)}, bf16[256,128]{1,0:T(8,128)(2,1)S(1)}, u32[]{:S(2)}, u32[]{:S(2)}) collective-permute-start(bf16[256,128]{1,0:T(8,128)(2,1)S(1)} %shard_map.89.refs_0_), channel_id=1, source_target_pairs={{0,2},{1,3},{2,0},{3,1},{4,6},{5,7},{6,4},{7,5},{8,10},{9,11},{10,... | collective-permute-start | bytes 196616 | tf_op jit(solution)/shard_map/ppermute | solution.py:87
  54.0 6.1 %collective-permute-start.11 = (bf16[256,128]{1,0:T(8,128)(2,1)S(1)}, bf16[256,128]{1,0:T(8,128)(2,1)S(1)}, u32[]{:S(2)}, u32[]{:S(2)}) collective-permute-start(bf16[256,128]{1,0:T(8,128)(2,1)S(1)} %shard_map.87.refs_0_), channel_id=1, source_target_pairs={{0,2},{1,3},{2,0},{3,1},{4,6},{5,7},{6,4},{7,5},{8,10},{9,11},{10,... | collective-permute-start | bytes 196616 | tf_op jit(solution)/shard_map/ppermute | solution.py:87
  54.6 5.5 %collective-permute-start.16 = (bf16[256,128]{1,0:T(8,128)(2,1)S(1)}, bf16[256,128]{1,0:T(8,128)(2,1)S(1)}, u32[]{:S(2)}, u32[]{:S(2)}) collective-permute-start(bf16[256,128]{1,0:T(8,128)(2,1)S(1)} %shard_map.89.refs_0_), channel_id=1, source_target_pairs={{0,1},{1,0},{2,3},{3,2},{4,5},{5,4},{6,7},{7,6},{8,9},{9,8},{10,11... | collective-permute-start | bytes 196616 | tf_op jit(solution)/shard_map/ppermute | solution.py:87
  59.0 1.3 %collective-permute-start.18 = (bf16[256,128]{1,0:T(8,128)(2,1)S(1)}, bf16[256,128]{1,0:T(8,128)(2,1)S(1)}, u32[]{:S(2)}, u32[]{:S(2)}) collective-permute-start(bf16[256,128]{1,0:T(8,128)(2,1)S(1)} %collective-permute-done.17.refs_2_), channel_id=1, source_target_pairs={{0,1},{1,0},{2,3},{3,2},{4,5},{5,4},{6,7},{7,6},{8,9},{9,8},{10,11... | collective-permute-start | bytes 196616 | tf_op jit(solution)/shard_map/ppermute | solution.py:87
  59.0 1.5 %collective-permute-start.10 = (bf16[256,128]{1,0:T(8,128)(2,1)S(1)}, bf16[256,128]{1,0:T(8,128)(2,1)S(1)}, u32[]{:S(2)}, u32[]{:S(2)}) collective-permute-start(bf16[256,128]{1,0:T(8,128)(2,1)S(1)} %shard_map.87.refs_0_), channel_id=1, source_target_pairs={{0,1},{1,0},{2,3},{3,2},{4,5},{5,4},{6,7},{7,6},{8,9},{9,8},{10,11... | collective-permute-start | bytes 196616 | tf_op jit(solution)/shard_map/ppermute | solution.py:87
  60.1 1.3 %collective-permute-start.12 = (bf16[256,128]{1,0:T(8,128)(2,1)S(1)}, bf16[256,128]{1,0:T(8,128)(2,1)S(1)}, u32[]{:S(2)}, u32[]{:S(2)}) collective-permute-start(bf16[256,128]{1,0:T(8,128)(2,1)S(1)} %collective-permute-done.11.refs_2_), channel_id=1, source_target_pairs={{0,1},{1,0},{2,3},{3,2},{4,5},{5,4},{6,7},{7,6},{8,9},{9,8},{10,11... | collective-permute-start | bytes 196616 | tf_op jit(solution)/shard_map/ppermute | solution.py:87

commit v2 on v1

--- a/solution.py
+++ b/solution.py
@@ -348,10 +348,10 @@
                 lead = raw * scale_len
                 weights = (lead + lead * jnp.tanh(raw * scale)).astype(jnp.bfloat16)
                 total += jnp.dot(weights, value, preferred_element_type=jnp.float32)
-        out_ref[:, cols] = total
-
-
-def attend(length, plan, queries, keys, values, events, group):
+        out_ref[:, cols] = total.astype(out_ref.dtype)
+
+
+def attend(length, plan, queries, keys, values, events, group, dtype):
     width = queries[0].shape[1]
     item_count = plan.shape[0] // (len(events) + 1)
     event_count = (len(events) + 1) * keys.shape[0]
@@ -359,7 +359,7 @@
     operands = (length, plan, *queries, keys, values, *events)
     return pl.pallas_call(
         functools.partial(attention_kernel, group, len(queries)),
-        out_shape=jax.ShapeDtypeStruct((item_count, width), jnp.float32),
+        out_shape=jax.ShapeDtypeStruct((item_count, width), dtype),
         in_specs=[vmem] * len(operands),
         out_specs=vmem,
         compiler_params=pltpu.CompilerParams(vmem_limit_bytes=24 << 20),
@@ -371,64 +371,67 @@
     )(*operands)
 
 
-def gate_kernel(part, part_count, stride, plan_ref, attended_ref, *refs):
-    gate_refs, out_ref = refs[:-1], refs[-1]
-    item_count = out_ref.shape[0]
-    count = stride // part_count
-    starts = [ref.shape[0] - stride + part * count for ref in gate_refs]
-    slots = [ref[at : at + count, :] for at, ref in zip(starts, gate_refs, strict=True)]
-    gates = pick(plan_ref[:item_count, :], stride, slots)
-    out_ref[...] = (attended_ref[...] * gates).astype(out_ref.dtype)
-
-
-def gate(plan, attended, gates, part, part_count):
-    stride = gates[0].shape[0]
+def gate_kernel(part_count, stride, plan_ref, *refs):
+    attended_refs, gate_refs, out_ref = refs[:part_count], refs[part_count:-1], refs[-1]
+    width = attended_refs[0].shape[1]
+    item_count, count = out_ref.shape[0], stride // part_count
+    for part, attended_ref in enumerate(attended_refs):
+        starts = [ref.shape[0] - stride + part * count for ref in gate_refs]
+        slots = [ref[at : at + count, :] for at, ref in zip(starts, gate_refs, strict=True)]
+        gates = pick(plan_ref[:item_count, :], stride, slots)
+        out_ref[:, part * width : (part + 1) * width] = (
+            attended_ref[...].astype(jnp.float32) * gates
+        ).astype(out_ref.dtype)
+
+
+def gate(plan, attended, gates):
+    item_count, width = attended[0].shape
+    part_count = len(attended)
     vmem = pl.BlockSpec(memory_space=pltpu.VMEM)
-    operands = (plan, attended, *gates)
-    return pl.pallas_call(
-        functools.partial(gate_kernel, part, part_count, stride),
-        out_shape=jax.ShapeDtypeStruct(attended.shape, jnp.bfloat16),
+    operands = (plan, *attended, *gates)
+    return pl.pallas_call(
+        functools.partial(gate_kernel, part_count, gates[0].shape[0]),
+        out_shape=jax.ShapeDtypeStruct((item_count, part_count * width), jnp.bfloat16),
         in_specs=[vmem] * len(operands),
         out_specs=vmem,
         compiler_params=pltpu.CompilerParams(vmem_limit_bytes=16 << 20),
         cost_estimate=pl.CostEstimate(
-            flops=2 * attended.size * len(gates) * gates[0].shape[0],
+            flops=2 * item_count * width * len(gates) * gates[0].shape[0],
             transcendentals=0,
-            bytes_accessed=6 * attended.size,
+            bytes_accessed=6 * item_count * width * part_count,
         ),
     )(*operands)
 
 
-def project_kernel(head_count, part, *refs):
+def project_kernel(head_count, part_count, *refs):
     pieces, weights = refs[:head_count], refs[head_count : 2 * head_count]
     out_ref = refs[-1]
-    width = pieces[0].shape[1]
-    wanted = lax.axis_index("ctx") ^ part
+    width = pieces[0].shape[1] // part_count
     chosen = []
     for ref in weights:
-        weight = ref[:width, :]
-        for other in range(1, ref.shape[0] // width):
-            rows = slice(other * width, (other + 1) * width)
-            weight = jnp.where(wanted == other, ref[rows, :], weight)
-        chosen.append(weight)
+        for part in range(part_count):
+            wanted = lax.axis_index("ctx") ^ part
+            weight = ref[:width, :]
+            for other in range(1, part_count):
+                rows = slice(other * width, (other + 1) * width)
+                weight = jnp.where(wanted == other, ref[rows, :], weight)
+            chosen.append(weight)
     total = jnp.dot(
         jnp.concatenate([piece[...] for piece in pieces], axis=1),
         jnp.concatenate(chosen, axis=0),
         preferred_element_type=jnp.float32,
     )
-    if len(refs) > 2 * head_count + 1:
-        total += refs[2 * head_count][...]
     out_ref[...] = total.astype(out_ref.dtype)
 
 
-def project_out(pieces, weights, part, before, dtype):
+def project_out(pieces, weights, part_count):
     item_count, width = pieces[0].shape
     cols = weights[0].shape[1]
     vmem = pl.BlockSpec(memory_space=pltpu.VMEM)
-    operands = (*pieces, *weights) + (() if before is None else (before,))
-    return pl.pallas_call(
-        functools.partial(project_kernel, len(pieces), part),
-        out_shape=jax.ShapeDtypeStruct((item_count, cols), dtype),
+    operands = (*pieces, *weights)
+    return pl.pallas_call(
+        functools.partial(project_kernel, len(pieces), part_count),
+        out_shape=jax.ShapeDtypeStruct((item_count, cols), jnp.bfloat16),
         in_specs=[vmem] * len(operands),
         out_specs=vmem,
         compiler_params=pltpu.CompilerParams(vmem_limit_bytes=16 << 20),
@@ -481,22 +484,19 @@
 
     attended = [None] * ctx_count
     for k in range(ctx_count - 1, -1, -1):
-        own = attend(length, plan, queries, key_rows, value_rows, events, k)
+        own = attend(
+            length, plan, queries, key_rows, value_rows, events, k, jnp.bfloat16 if k else jnp.float32
+        )
         attended[k] = swap(own, "ctx", k) if k > 0 else own
 
-    ranked = None
-    for k in range(ctx_count):
-        gated = gate(plan, attended[k], gates, k, ctx_count)
-        parts, bit = {0: gated}, head_count // 2
-        while bit:
-            for j in list(parts):
-                parts[j ^ bit] = swap(parts[j], "head", bit)
-            bit //= 2
-        dtype = jnp.bfloat16 if k == ctx_count - 1 else jnp.float32
-        heads = range(head_count)
-        ranked = project_out(
-            [parts[j] for j in heads], [weights[j] for j in heads], k, ranked, dtype
-        )
+    gated = gate(plan, attended, gates)
+    parts, bit = {0: gated}, head_count // 2
+    while bit:
+        for j in list(parts):
+            parts[j ^ bit] = swap(parts[j], "head", bit)
+        bit //= 2
+    heads = range(head_count)
+    ranked = project_out([parts[j] for j in heads], [weights[j] for j in heads], ctx_count)
     return ranked.reshape(1, cand_count, col_share)
 
 

time: 62.4 us -> 62.8 us (level)
  waiting for transfers between devices: 26.5 us -> 28.2 us
  starting transfers between devices: 24.9 us -> 24.1 us
    ppermute x19 -> x16, waiting for transfers between devices: 26.5 us -> 28.2 us  [swap(): lax.ppermute(x, axis, [(i, i ^ k) for i in range(lax.axis_size(axis))])]
    ppermute x19 -> x16, starting transfers between devices: 24.9 us -> 24.1 us  [swap(): lax.ppermute(x, axis, [(i, i ^ k) for i in range(lax.axis_size(axis))])]
    pallas_call x4 -> x2, Pallas kernels: 1.79 us -> 1.43 us  [the longest x1 0.97 us: project_out(): pl.pallas_call(functools.partial(project_kernel, len(pieces), part_count)...]
  transfers between devices with their start and end apart: 19 -> 16, of which waited for: 8 -> 8; matrix products, arithmetic and copies ran while one was open for 0% -> 0% of each run, Pallas kernels for 11% -> 9%
where the time goes in v2:
time: 62.8 us; the launch traced here: 62.7 us
  waiting for transfers between devices  28.2 us (45%)
  starting transfers between devices  24.1 us (38%)
  Pallas kernels  9.27 us (15%)
  between operations  0.78 us (1%)
    ppermute x16, waiting for transfers between devices, swap(): lax.ppermute(x, axis, [(i, i ^ k) for i in range(lax.axis_size(axis))])  28.2 us
    ppermute x16, starting transfers between devices, swap(): lax.ppermute(x, axis, [(i, i ^ k) for i in range(lax.axis_size(axis))])  24.1 us
    pallas_call x2, Pallas kernels, attend(): pl.pallas_call(functools.partial(attention_kernel, group, len(queries)),...  3.02 us
    pallas_call x1, Pallas kernels, split_events(): pl.pallas_call(functools.partial(split_kernel, partner), out_shape=jax.Sh...  2.04 us
    pallas_call x1, Pallas kernels, serve(): pl.pallas_call(functools.partial(serve_kernel, len(pieces), user_count, s...  1.42 us
  transfers between devices with their start and end apart: 16, of which 8 were waited for; matrix products, arithmetic and copies ran while one was open for 0% of the time, Pallas kernels for 9%

profile of v2, /device:TPU:0, one launch (start us, length us, event | category | flops | bytes accessed | tf_op | source)
XLA Modules:
  0.0 62.7 jit_solution(18057405174663842700)
XLA Ops:
  0.0 2.0 %shard_map.85 = bf16[3072,128]{1,0:T(8,128)(2,1)} custom-call(bf16[1536,256]{1,0:T(8,128)(2,1)} %bitcast.10, bf16[1536,256]{1,0:T(8,128)(2,1)} %bitcast.13), custom_call_target="tpu_custom_call" | custom-call | bytes 1572864 | tf_op jit(solution)/shard_map/pallas_call | solution.py:134
  2.1 3.1 %collective-permute-start.6 = (bf16[3072,128]{1,0:T(8,128)(2,1)}, bf16[3072,128]{1,0:T(8,128)(2,1)S(1)}, u32[]{:S(2)}, u32[]{:S(2)}) collective-permute-start(bf16[3072,128]{1,0:T(8,128)(2,1)} %shard_map.85), channel_id=1, source_target_pairs={{0,4},{4,0},{1,5},{5,1},{2,6},{6,2},{3,7},{7,3},{8,12},{12,8},{9,1... | collective-permute-start | bytes 2359304 | tf_op jit(solution)/shard_map/ppermute | solution.py:87
  5.1 0.0 copy-done.5
  5.1 0.1 collective-permute-start
  5.2 17.7 %collective-permute-done = s32[1,256]{1,0:T(1,128)S(1)} collective-permute-done((s32[1,256]{1,0:T(1,128)S(1)}, s32[1,256]{1,0:T(1,128)S(1)}, u32[]{:S(2)}, u32[]{:S(2)}) %collective-permute-start) | collective-permute-done | bytes 1056 | tf_op jit(solution)/shard_map/ppermute | solution.py:87
  23.0 1.8 %collective-permute-start.1 = (s32[1,512]{1,0:T(1,128)S(1)}, s32[1,512]{1,0:T(1,128)S(1)}, u32[]{:S(2)}, u32[]{:S(2)}) collective-permute-start(s32[1,512]{1,0:T(1,128)S(1)} %pad_add_fusion.1.refs_0_), channel_id=1, source_target_pairs={{0,8},{8,0},{16,24},{24,16},{1,9},{9,1},{17,25},{25,17},{2,10},{10... | collective-permute-start | bytes 6152 | tf_op jit(solution)/shard_map/ppermute | solution.py:87
  24.8 0.0 copy-done.3
  24.8 0.2 copy.9
  25.0 1.6 %collective-permute-done.1.refs_1_ = s32[1,512]{1,0:T(1,128)S(1)} collective-permute-done((s32[1,512]{1,0:T(1,128)S(1)}, s32[1,512]{1,0:T(1,128)S(1)}, u32[]{:S(2)}, u32[]{:S(2)}) %collective-permute-start.1) | collective-permute-done | bytes 2080 | tf_op jit(solution)/shard_map/ppermute | solution.py:87
  26.5 2.9 %collective-permute-start.2 = (s32[2,512]{1,0:T(2,128)S(1)}, s32[2,512]{1,0:T(2,128)S(1)}, u32[]{:S(2)}, u32[]{:S(2)}) collective-permute-start(s32[2,512]{1,0:T(2,128)S(1)} %pad_add_fusion), channel_id=1, source_target_pairs={{0,16},{8,24},{16,0},{24,8},{1,17},{9,25},{17,1},{25,9},{2,18},{10... | collective-permute-start | bytes 12296 | tf_op jit(solution)/shard_map/ppermute | solution.py:87
  29.4 0.0 copy-done.2
  29.4 0.8 %shard_map.82 = (bf16[512,128]{1,0:T(8,128)(2,1)S(1)}, bf16[512,256]{1,0:T(8,128)(2,1)S(1)}) custom-call(bf16[512,1024]{1,0:T(8,128)(2,1)S(1)} %copy-done.2, bf16[1024,512]{1,0:T(8,128)(2,1)S(1)} %bitcast.16), custom_call_target="tpu_custom_call" | custom-call | flops 402653184 | bytes 2097152 | tf_op jit(solution)/shard_map/pallas_call | solution.py:164
  30.2 0.0 copy-start
  30.2 0.9 %collective-permute-done.2.refs_2_ = s32[2,512]{1,0:T(2,128)S(1)} collective-permute-done((s32[2,512]{1,0:T(2,128)S(1)}, s32[2,512]{1,0:T(2,128)S(1)}, u32[]{:S(2)}, u32[]{:S(2)}) %collective-permute-start.2) | collective-permute-done | bytes 4128 | tf_op jit(solution)/shard_map/ppermute | solution.py:87
  31.1 1.4 %shard_map.83 = (s32[256,4]{1,0:T(8,128)S(1)}, f32[2,512]{1,0:T(2,128)S(1)}, bf16[512,128]{1,0:T(8,128)(2,1)S(1)}, bf16[256,128]{1,0:T(8,128)(2,1)S(1)}, bf16[256,128]{1,0:T(8,128)(2,1)S(1)}) custom-call(s32[1,512]{1,0:T(1,128)S(1)} %pad_add_fusion.1.refs_0_, s32[1,512]{1,0:T(1,128)S(1)} %collective-permute-done.1.refs_1_, ...), custom_call_target="tpu_custom_call" | custom-call | flops 134217728 | bytes 131072 | tf_op jit(solution)/shard_map/pallas_call | solution.py:239
  32.5 1.9 %collective-permute-start.3 = (bf16[512,128]{1,0:T(8,128)(2,1)S(1)}, bf16[512,128]{1,0:T(8,128)(2,1)S(1)}, u32[]{:S(2)}, u32[]{:S(2)}) collective-permute-start(bf16[512,128]{1,0:T(8,128)(2,1)S(1)} %get-tuple-element.23), channel_id=1, source_target_pairs={{0,8},{8,0},{16,24},{24,16},{1,9},{9,1},{17,25},{25,17},{2,10},{10... | collective-permute-start | bytes 393224 | tf_op jit(solution)/shard_map/ppermute | solution.py:87
  34.4 2.6 %collective-permute-start.4 = (bf16[256,128]{1,0:T(8,128)(2,1)S(1)}, bf16[256,128]{1,0:T(8,128)(2,1)S(1)}, u32[]{:S(2)}, u32[]{:S(2)}) collective-permute-start(bf16[256,128]{1,0:T(8,128)(2,1)S(1)} %get-tuple-element.24), channel_id=1, source_target_pairs={{0,16},{8,24},{16,0},{24,8},{1,17},{9,25},{17,1},{25,9},{2,18},{10... | collective-permute-start | bytes 196616 | tf_op jit(solution)/shard_map/ppermute | solution.py:87
  37.0 0.0 collective-permute-start.5
  37.7 0.6 shard_map.84
  38.3 2.0 %collective-permute-start.8 = (bf16[256,128]{1,0:T(8,128)(2,1)S(1)}, bf16[256,128]{1,0:T(8,128)(2,1)S(1)}, u32[]{:S(2)}, u32[]{:S(2)}) collective-permute-start(bf16[256,128]{1,0:T(8,128)(2,1)S(1)} %get-tuple-element.27), channel_id=1, source_target_pairs={{0,16},{8,24},{16,0},{24,8},{1,17},{9,25},{17,1},{25,9},{2,18},{10... | collective-permute-start | bytes 196616 | tf_op jit(solution)/shard_map/ppermute | solution.py:87
  40.2 0.4 collective-permute-done.4.refs_2_
  40.6 4.4 %collective-permute-start.9 = (bf16[256,128]{1,0:T(8,128)(2,1)S(1)}, bf16[256,128]{1,0:T(8,128)(2,1)S(1)}, u32[]{:S(2)}, u32[]{:S(2)}) collective-permute-start(bf16[256,128]{1,0:T(8,128)(2,1)S(1)} %get-tuple-element.28), channel_id=1, source_target_pairs={{0,24},{8,16},{16,8},{24,0},{1,25},{9,17},{17,9},{25,1},{2,26},{10... | collective-permute-start | bytes 196616 | tf_op jit(solution)/shard_map/ppermute | solution.py:87
  45.0 0.0 collective-permute-done.5.refs_3_
  45.0 0.0 collective-permute-done.3.refs_1_.refs_3_
  45.0 0.0 collective-permute-done.6.refs_6_
  45.1 1.5 %shard_map.87 = bf16[256,128]{1,0:T(8,128)(2,1)S(1)} custom-call(s32[1,1]{1,0:T(1,128)} %bitcast.9.length_ref, s32[512,1]{1,0:T(8,128)S(1)} %get-tuple-element.21.plan_ref, bf16[256,128]{1,0:T(8,128)(2,1)S(1)} %get-tuple-element.22.refs_0_, bf16[512,128]{1,0:T(8,128)(2,1)S(1)} %collective-permute-done.3.refs_1_.refs_3_, ...), custom_call_target="tpu_custom_call" | custom-call | flops 402653184 | bytes 1572864 | tf_op jit(solution)/shard_map/pallas_call | solution.py:360
  46.6 1.6 %collective-permute-start.7 = (bf16[256,128]{1,0:T(8,128)(2,1)S(1)}, bf16[256,128]{1,0:T(8,128)(2,1)S(1)}, u32[]{:S(2)}, u32[]{:S(2)}) collective-permute-start(bf16[256,128]{1,0:T(8,128)(2,1)S(1)} %shard_map.87), channel_id=1, source_target_pairs={{0,4},{4,0},{1,5},{5,1},{2,6},{6,2},{3,7},{7,3},{8,12},{12,8},{9,1... | collective-permute-start | bytes 196616 | tf_op jit(solution)/shard_map/ppermute | solution.py:87
  48.2 1.5 %shard_map.86.refs_0_ = f32[256,128]{1,0:T(8,128)S(1)} custom-call(s32[1,1]{1,0:T(1,128)} %bitcast.8.length_ref, s32[512,1]{1,0:T(8,128)S(1)} %get-tuple-element.21.plan_ref, bf16[256,128]{1,0:T(8,128)(2,1)S(1)} %get-tuple-element.22.refs_0_, bf16[512,128]{1,0:T(8,128)(2,1)S(1)} %collective-permute-done.3.refs_1_.refs_3_, ...), custom_call_target="tpu_custom_call" | custom-call | flops 402653184 | bytes 1572864 | tf_op jit(solution)/shard_map/pallas_call | solution.py:360
  49.7 0.0 copy-start.4
  49.7 0.0 collective-permute-done.8.refs_4_
  49.7 0.0 collective-permute-done.9.refs_5_
  49.7 1.2 %collective-permute-done.7.refs_1_ = bf16[256,128]{1,0:T(8,128)(2,1)S(1)} collective-permute-done((bf16[256,128]{1,0:T(8,128)(2,1)S(1)}, bf16[256,128]{1,0:T(8,128)(2,1)S(1)}, u32[]{:S(2)}, u32[]{:S(2)}) %collective-permute-start.7) | collective-permute-done | bytes 65568 | tf_op jit(solution)/shard_map/ppermute | solution.py:87
  50.9 0.5 shard_map.88.refs_0_
  51.4 1.6 %collective-permute-start.11 = (bf16[256,256]{1,0:T(8,128)(2,1)S(1)}, bf16[256,256]{1,0:T(8,128)(2,1)S(1)}, u32[]{:S(2)}, u32[]{:S(2)}) collective-permute-start(bf16[256,256]{1,0:T(8,128)(2,1)S(1)} %shard_map.88.refs_0_), channel_id=1, source_target_pairs={{0,2},{1,3},{2,0},{3,1},{4,6},{5,7},{6,4},{7,5},{8,10},{9,11},{10,... | collective-permute-start | bytes 393224 | tf_op jit(solution)/shard_map/ppermute | solution.py:87
  53.0 0.0 copy-done.4
  53.0 0.1 constant_dynamic-slice_fusion
  53.0 0.1 collective-permute-start.13
  53.1 0.6 collective-permute-start.14
  53.7 1.3 %collective-permute-start.15 = (bf16[256,256]{1,0:T(8,128)(2,1)S(1)}, bf16[256,256]{1,0:T(8,128)(2,1)S(1)}, u32[]{:S(2)}, u32[]{:S(2)}) collective-permute-start(bf16[256,256]{1,0:T(8,128)(2,1)S(1)} %get-tuple-element.29), channel_id=1, source_target_pairs={{0,3},{1,2},{2,1},{3,0},{4,7},{5,6},{6,5},{7,4},{8,11},{9,10},{10,... | collective-permute-start | bytes 393224 | tf_op jit(solution)/shard_map/ppermute | solution.py:87
  55.0 0.4 collective-permute-start.10
  55.3 1.3 %collective-permute-done.11.refs_2_ = bf16[256,256]{1,0:T(8,128)(2,1)S(1)} collective-permute-done((bf16[256,256]{1,0:T(8,128)(2,1)S(1)}, bf16[256,256]{1,0:T(8,128)(2,1)S(1)}, u32[]{:S(2)}, u32[]{:S(2)}) %collective-permute-start.11) | collective-permute-done | bytes 131104 | tf_op jit(solution)/shard_map/ppermute | solution.py:87
  56.6 0.0 collective-permute-start.12
  56.6 0.0 collective-permute-done.13.refs_5_
  56.6 2.9 %collective-permute-done.14.refs_6_ = bf16[256,256]{1,0:T(8,128)(2,1)S(1)} collective-permute-done((bf16[256,256]{1,0:T(8,128)(2,1)S(1)}, bf16[256,256]{1,0:T(8,128)(2,1)S(1)}, u32[]{:S(2)}, u32[]{:S(2)}) %collective-permute-start.14) | collective-permute-done | bytes 131104 | tf_op jit(solution)/shard_map/ppermute | solution.py:87
  59.5 2.2 %collective-permute-done.15.refs_7_ = bf16[256,256]{1,0:T(8,128)(2,1)S(1)} collective-permute-done((bf16[256,256]{1,0:T(8,128)(2,1)S(1)}, bf16[256,256]{1,0:T(8,128)(2,1)S(1)}, u32[]{:S(2)}, u32[]{:S(2)}) %collective-permute-start.15) | collective-permute-done | bytes 131104 | tf_op jit(solution)/shard_map/ppermute | solution.py:87
  61.7 0.0 collective-permute-done.10.refs_1_
  61.7 0.0 collective-permute-done.12.refs_3_
  61.7 1.0 %shard_map.89 = bf16[256,256]{1,0:T(8,128)(2,1)} custom-call(bf16[256,256]{1,0:T(8,128)(2,1)S(1)} %shard_map.88.refs_0_, bf16[256,256]{1,0:T(8,128)(2,1)S(1)} %collective-permute-done.10.refs_1_, bf16[256,256]{1,0:T(8,128)(2,1)S(1)} %collective-permute-done.11.refs_2_, bf16[256,256]{1,0:T(8,128)(2,1)S(1)} %collective-permute-done.12.refs_3_, ...), custom_call_target="tpu_custom_call" | custom-call | flops 134217728 | bytes 524288 | tf_op jit(solution)/shard_map/pallas_call | solution.py:432
  (11 shorter events, 0.0 us)
Async XLA Ops:
  0.0 5.1 %copy-start.5 = (s32[1,256]{1,0:T(1,128)S(1)}, s32[1,256]{1,0:T(1,128)}, u32[]{:S(2)}) copy-start(s32[1,256]{1,0:T(1,128)} %param.10) | copy-start | bytes 3076
  0.0 5.1 %copy-start.6 = (s32[1,256,1]{1,2,0:T(1,128)S(1)}, s32[1,256,1]{1,2,0:T(1,128)}, u32[]{:S(2)}) copy-start(s32[1,256,1]{1,2,0:T(1,128)} %param.9) | copy-start | bytes 3076
  0.0 24.7 %copy-start.3 = (bf16[1024,2,256]{2,1,0:T(2,128)(2,1)S(1)}, bf16[1024,2,256]{2,1,0:T(2,128)(2,1)}, u32[]{:S(2)}) copy-start(bf16[1024,2,256]{2,1,0:T(2,128)(2,1)} %param.12) | copy-start | bytes 3145732
  2.1 43.0 %collective-permute-start.6 = (bf16[3072,128]{1,0:T(8,128)(2,1)}, bf16[3072,128]{1,0:T(8,128)(2,1)S(1)}, u32[]{:S(2)}, u32[]{:S(2)}) collective-permute-start(bf16[3072,128]{1,0:T(8,128)(2,1)} %shard_map.85), channel_id=1, source_target_pairs={{0,4},{4,0},{1,5},{5,1},{2,6},{6,2},{3,7},{7,3},{8,12},{12,8},{9,1... | collective-permute-start | bytes 2359304 | tf_op jit(solution)/shard_map/ppermute | solution.py:87
  5.1 17.8 %collective-permute-start = (s32[1,256]{1,0:T(1,128)S(1)}, s32[1,256]{1,0:T(1,128)S(1)}, u32[]{:S(2)}, u32[]{:S(2)}) collective-permute-start(s32[1,256]{1,0:T(1,128)S(1)} %bitcast_add_fusion), channel_id=1, source_target_pairs={{0,4},{4,0},{1,5},{5,1},{2,6},{6,2},{3,7},{7,3},{8,12},{12,8},{9,1... | collective-permute-start | bytes 3080 | tf_op jit(solution)/shard_map/ppermute | solution.py:87
  23.0 3.6 %collective-permute-start.1 = (s32[1,512]{1,0:T(1,128)S(1)}, s32[1,512]{1,0:T(1,128)S(1)}, u32[]{:S(2)}, u32[]{:S(2)}) collective-permute-start(s32[1,512]{1,0:T(1,128)S(1)} %pad_add_fusion.1.refs_0_), channel_id=1, source_target_pairs={{0,8},{8,0},{16,24},{24,16},{1,9},{9,1},{17,25},{25,17},{2,10},{10... | collective-permute-start | bytes 6152 | tf_op jit(solution)/shard_map/ppermute | solution.py:87
  24.8 4.7 %copy-start.2 = (bf16[512,1024]{1,0:T(8,128)(2,1)S(1)}, bf16[512,1024]{1,0:T(8,128)(2,1)}, u32[]{:S(2)}) copy-start(bf16[512,1024]{1,0:T(8,128)(2,1)} %catalog_ref.1) | copy-start | bytes 3145732
  26.5 4.6 %collective-permute-start.2 = (s32[2,512]{1,0:T(2,128)S(1)}, s32[2,512]{1,0:T(2,128)S(1)}, u32[]{:S(2)}, u32[]{:S(2)}) collective-permute-start(s32[2,512]{1,0:T(2,128)S(1)} %pad_add_fusion), channel_id=1, source_target_pairs={{0,16},{8,24},{16,0},{24,8},{1,17},{9,25},{17,1},{25,9},{2,18},{10... | collective-permute-start | bytes 12296 | tf_op jit(solution)/shard_map/ppermute | solution.py:87
  29.4 15.6 %copy-start.1 = (bf16[1,1536,256]{2,1,0:T(8,128)(2,1)S(1)}, bf16[1,1536,256]{2,1,0:T(8,128)(2,1)}, u32[]{:S(2)}) copy-start(bf16[1,1536,256]{2,1,0:T(8,128)(2,1)} %param.14) | copy-start | bytes 2359300
  30.2 14.9 %copy-start = (bf16[1,1536,256]{2,1,0:T(8,128)(2,1)S(1)}, bf16[1,1536,256]{2,1,0:T(8,128)(2,1)}, u32[]{:S(2)}) copy-start(bf16[1,1536,256]{2,1,0:T(8,128)(2,1)} %param.13) | copy-start | bytes 2359300
  32.5 12.5 %collective-permute-start.3 = (bf16[512,128]{1,0:T(8,128)(2,1)S(1)}, bf16[512,128]{1,0:T(8,128)(2,1)S(1)}, u32[]{:S(2)}, u32[]{:S(2)}) collective-permute-start(bf16[512,128]{1,0:T(8,128)(2,1)S(1)} %get-tuple-element.23), channel_id=1, source_target_pairs={{0,8},{8,0},{16,24},{24,16},{1,9},{9,1},{17,25},{25,17},{2,10},{10... | collective-permute-start | bytes 393224 | tf_op jit(solution)/shard_map/ppermute | solution.py:87
  34.4 6.2 %collective-permute-start.4 = (bf16[256,128]{1,0:T(8,128)(2,1)S(1)}, bf16[256,128]{1,0:T(8,128)(2,1)S(1)}, u32[]{:S(2)}, u32[]{:S(2)}) collective-permute-start(bf16[256,128]{1,0:T(8,128)(2,1)S(1)} %get-tuple-element.24), channel_id=1, source_target_pairs={{0,16},{8,24},{16,0},{24,8},{1,17},{9,25},{17,1},{25,9},{2,18},{10... | collective-permute-start | bytes 196616 | tf_op jit(solution)/shard_map/ppermute | solution.py:87
  37.0 8.0 %collective-permute-start.5 = (bf16[256,128]{1,0:T(8,128)(2,1)S(1)}, bf16[256,128]{1,0:T(8,128)(2,1)S(1)}, u32[]{:S(2)}, u32[]{:S(2)}) collective-permute-start(bf16[256,128]{1,0:T(8,128)(2,1)S(1)} %get-tuple-element.25), channel_id=1, source_target_pairs={{0,24},{8,16},{16,8},{24,0},{1,25},{9,17},{17,9},{25,1},{2,26},{10... | collective-permute-start | bytes 196616 | tf_op jit(solution)/shard_map/ppermute | solution.py:87
  38.3 11.4 %collective-permute-start.8 = (bf16[256,128]{1,0:T(8,128)(2,1)S(1)}, bf16[256,128]{1,0:T(8,128)(2,1)S(1)}, u32[]{:S(2)}, u32[]{:S(2)}) collective-permute-start(bf16[256,128]{1,0:T(8,128)(2,1)S(1)} %get-tuple-element.27), channel_id=1, source_target_pairs={{0,16},{8,24},{16,0},{24,8},{1,17},{9,25},{17,1},{25,9},{2,18},{10... | collective-permute-start | bytes 196616 | tf_op jit(solution)/shard_map/ppermute | solution.py:87
  40.6 9.1 %collective-permute-start.9 = (bf16[256,128]{1,0:T(8,128)(2,1)S(1)}, bf16[256,128]{1,0:T(8,128)(2,1)S(1)}, u32[]{:S(2)}, u32[]{:S(2)}) collective-permute-start(bf16[256,128]{1,0:T(8,128)(2,1)S(1)} %get-tuple-element.28), channel_id=1, source_target_pairs={{0,24},{8,16},{16,8},{24,0},{1,25},{9,17},{17,9},{25,1},{2,26},{10... | collective-permute-start | bytes 196616 | tf_op jit(solution)/shard_map/ppermute | solution.py:87
  46.6 4.3 %collective-permute-start.7 = (bf16[256,128]{1,0:T(8,128)(2,1)S(1)}, bf16[256,128]{1,0:T(8,128)(2,1)S(1)}, u32[]{:S(2)}, u32[]{:S(2)}) collective-permute-start(bf16[256,128]{1,0:T(8,128)(2,1)S(1)} %shard_map.87), channel_id=1, source_target_pairs={{0,4},{4,0},{1,5},{5,1},{2,6},{6,2},{3,7},{7,3},{8,12},{12,8},{9,1... | collective-permute-start | bytes 196616 | tf_op jit(solution)/shard_map/ppermute | solution.py:87
  49.7 3.3 %copy-start.4 = (bf16[256,1024]{1,0:T(8,128)(2,1)S(1)}, bf16[256,1024]{1,0:T(8,128)(2,1)}, u32[]{:S(2)}) copy-start(bf16[256,1024]{1,0:T(8,128)(2,1)} %param.15) | copy-start | bytes 1572868
  51.4 5.3 %collective-permute-start.11 = (bf16[256,256]{1,0:T(8,128)(2,1)S(1)}, bf16[256,256]{1,0:T(8,128)(2,1)S(1)}, u32[]{:S(2)}, u32[]{:S(2)}) collective-permute-start(bf16[256,256]{1,0:T(8,128)(2,1)S(1)} %shard_map.88.refs_0_), channel_id=1, source_target_pairs={{0,2},{1,3},{2,0},{3,1},{4,6},{5,7},{6,4},{7,5},{8,10},{9,11},{10,... | collective-permute-start | bytes 393224 | tf_op jit(solution)/shard_map/ppermute | solution.py:87
  53.0 3.6 %collective-permute-start.13 = (bf16[256,256]{1,0:T(8,128)(2,1)S(1)}, bf16[256,256]{1,0:T(8,128)(2,1)S(1)}, u32[]{:S(2)}, u32[]{:S(2)}) collective-permute-start(bf16[256,256]{1,0:T(8,128)(2,1)S(1)} %get-tuple-element.30), channel_id=1, source_target_pairs={{0,1},{1,0},{2,3},{3,2},{4,5},{5,4},{6,7},{7,6},{8,9},{9,8},{10,11... | collective-permute-start | bytes 393224 | tf_op jit(solution)/shard_map/ppermute | solution.py:87
  53.1 6.4 %collective-permute-start.14 = (bf16[256,256]{1,0:T(8,128)(2,1)S(1)}, bf16[256,256]{1,0:T(8,128)(2,1)S(1)}, u32[]{:S(2)}, u32[]{:S(2)}) collective-permute-start(bf16[256,256]{1,0:T(8,128)(2,1)S(1)} %get-tuple-element.32), channel_id=1, source_target_pairs={{0,2},{1,3},{2,0},{3,1},{4,6},{5,7},{6,4},{7,5},{8,10},{9,11},{10,... | collective-permute-start | bytes 393224 | tf_op jit(solution)/shard_map/ppermute | solution.py:87
  53.7 8.0 %collective-permute-start.15 = (bf16[256,256]{1,0:T(8,128)(2,1)S(1)}, bf16[256,256]{1,0:T(8,128)(2,1)S(1)}, u32[]{:S(2)}, u32[]{:S(2)}) collective-permute-start(bf16[256,256]{1,0:T(8,128)(2,1)S(1)} %get-tuple-element.29), channel_id=1, source_target_pairs={{0,3},{1,2},{2,1},{3,0},{4,7},{5,6},{6,5},{7,4},{8,11},{9,10},{10,... | collective-permute-start | bytes 393224 | tf_op jit(solution)/shard_map/ppermute | solution.py:87
  55.0 6.8 %collective-permute-start.10 = (bf16[256,256]{1,0:T(8,128)(2,1)S(1)}, bf16[256,256]{1,0:T(8,128)(2,1)S(1)}, u32[]{:S(2)}, u32[]{:S(2)}) collective-permute-start(bf16[256,256]{1,0:T(8,128)(2,1)S(1)} %shard_map.88.refs_0_), channel_id=1, source_target_pairs={{0,1},{1,0},{2,3},{3,2},{4,5},{5,4},{6,7},{7,6},{8,9},{9,8},{10,11... | collective-permute-start | bytes 393224 | tf_op jit(solution)/shard_map/ppermute | solution.py:87
  56.6 5.1 %collective-permute-start.12 = (bf16[256,256]{1,0:T(8,128)(2,1)S(1)}, bf16[256,256]{1,0:T(8,128)(2,1)S(1)}, u32[]{:S(2)}, u32[]{:S(2)}) collective-permute-start(bf16[256,256]{1,0:T(8,128)(2,1)S(1)} %collective-permute-done.11.refs_2_), channel_id=1, source_target_pairs={{0,1},{1,0},{2,3},{3,2},{4,5},{5,4},{6,7},{7,6},{8,9},{9,8},{10,11... | collective-permute-start | bytes 393224 | tf_op jit(solution)/shard_map/ppermute | solution.py:87
